TPU v7x, 32 devices: a whole 2x2x4 slice. The times are simulated.
32 devices in a mesh: node: 8 (over z, y), rep: 4 (over x, core).
Axes of the slice: x: 2, y: 2, z: 4, core: 2. Of those that a mesh axis runs over, the one named last changes fastest.
Arguments:
- tokens: bfloat16 [4096, 8192], P(('node', 'rep')), may hold values from -6 to 6
- norm_gain: float32 [8192], replicated, may hold values from 0.5 to 1.5
- key_cotangent: bfloat16 [4096, 512], P(('node', 'rep')), may hold values from -6 to 6
- secondary: bfloat16 [8192, 512], P('node'), may hold values from -0.0625 to 0.0625
- master: float32 [8192, 512], P(('node', 'rep')), may hold values from -0.0625 to 0.0625
- moment_first: float32 [4096, 1024], P(('node', 'rep')), may hold values from -0.09375 to 0.09375
- moment_second: float32 [4096, 1024], P(('node', 'rep')), may hold values from 6.1035156e-05 to 0.0009765625
- signs: int32 [1024], replicated, may hold values from 0 to 1
Outputs:
- keys: bfloat16 [4096, 512], P(('node', 'rep'))
- token_grad: bfloat16 [4096, 8192], P(('node', 'rep'))
- new_master: float32 [8192, 512], P(('node', 'rep'))
- new_first: float32 [4096, 1024], P(('node', 'rep'))
- new_second: float32 [4096, 1024], P(('node', 'rep'))
- new_secondary: bfloat16 [8192, 512], P('node')
All inputs are finite; a program needn't handle non-finite values.
Results may differ from a plain program's by a relative error of at most 0.0049.
Values may be sent and summed in bfloat16 or wider, within the bound.
A program may use at most 128 MiB of HBM per device.

v0:
```python
import functools
import math

import jax
import jax.numpy as jnp
from jax import lax
from jax.experimental import pallas as pl
from jax.experimental.pallas import tpu as pltpu
from jax.sharding import PartitionSpec as P

PAIR_GAP = 16
MESH = pl.DeviceIdType.MESH

norm_eps = 1e-05
adam_eps = 1e-08
beta_first = 0.9
beta_second = 0.95
adam_steps = 10
learn_rate = 0.002
weight_decay = 0.1

ANY = pl.BlockSpec(memory_space=pl.ANY)
VMEM = pl.BlockSpec(memory_space=pltpu.VMEM)


def sylvester(extent):
    position = jnp.arange(extent, dtype=jnp.int32)
    parity = jnp.zeros((extent, extent), jnp.int32)
    for bit_place in range(extent.bit_length() - 1):
        parity = parity + (position[:, None] >> bit_place & 1) * (
            position[None, :] >> bit_place & 1
        )
    return (1 - 2 * (parity % 2)).astype(jnp.float32)


def split(index):
    return index // 2, lax.rem(index, 2)


def greet(peers):
    barrier = pltpu.get_barrier_semaphore()
    for peer in peers:
        pl.semaphore_signal(barrier, inc=1, device_id=peer, device_id_type=MESH)
    pl.semaphore_wait(barrier, len(peers))


def remote(src, dst, send, recv, peer):
    return pltpu.make_async_remote_copy(
        src_ref=src,
        dst_ref=dst,
        send_sem=send,
        recv_sem=recv,
        device_id=peer,
        device_id_type=MESH,
    )


def axis_peers(axis, size):
    me = lax.axis_index(axis)
    return [{axis: lax.rem(me + k, size)} for k in range(1, size)]


def pair_peers(axis, size):
    high, low = split(lax.axis_index(axis))
    half = size // 2
    partner = {axis: high * 2 + 1 - low}
    same = [{axis: lax.rem(high + k, half) * 2 + low} for k in range(1, half)]
    return partner, same


class PairGather:
    def __init__(self, axis, size, src, out, local_sem, send, recv):
        self.half = size // 2
        me = lax.axis_index(axis)
        high, low = split(me)
        partner, same = pair_peers(axis, size)
        self.local = pltpu.make_async_copy(src, out.at[me], local_sem)
        self.first = [
            remote(src, out.at[me], send.at[0, k], recv.at[0, k], same[k - 1])
            for k in range(1, self.half)
        ]
        self.second = [remote(src, out.at[me], send.at[1, 0], recv.at[1, 0], partner)]
        for k in range(1, self.half):
            origin = lax.rem(high + self.half - k, self.half) * 2 + low
            self.second.append(
                remote(out.at[origin], out.at[origin], send.at[1, k], recv.at[1, k], partner)
            )

    def start(self):
        for copy in self.first:
            copy.start()
        self.second[0].start()
        self.local.start()

    def forward(self, k):
        self.first[k - 1].wait_recv()
        self.second[k].start()

    def finish(self):
        for copy in self.second:
            copy.wait_recv()
        for copy in self.first + self.second:
            copy.wait_send()
        self.local.wait()


def step_kernel(
    nodes, reps, aligned, scale, hid, cot, sec, table, coded, keys, grad_out,
    hid_in, cot_in, sec_in, rot, term, grad, acc, part,
    from_pair, to_same, from_same, key_in,
    cs, cr, hs, hr, ss, sr, ps, pr, zs, zr, gs, gr, ks, kr, cot_own, hid_own, sec_own, grad_own,
):
    f32 = jnp.float32
    rep = lax.axis_index("rep")
    high, low = split(lax.axis_index("node"))
    half = nodes // 2
    partner, same = pair_peers("node", nodes)
    rep_peers = axis_peers("rep", reps)
    columns, key_width = sec_in.shape[1:]
    tok_rows = cot_in.shape[1]
    group_tokens = reps * tok_rows

    def piece(ref, node, owner):
        index = node * reps + owner
        if aligned:
            return ref.at[:, pl.ds(pl.multiple_of(index * columns, columns), columns)]
        return ref.at[index]

    greet(rep_peers + [partner] + same)
    weights = PairGather(
        "node", nodes, sec.at[pl.ds(pl.multiple_of(rep * columns, columns), columns)], sec_in,
        sec_own.at[0], ss, sr,
    )
    weights.start()
    cot_moves = [
        remote(cot, cot_in.at[rep], cs.at[k], cr.at[k], peer) for k, peer in enumerate(rep_peers)
    ]
    cot_moves.append(pltpu.make_async_copy(cot, cot_in.at[rep], cot_own.at[0]))
    for copy in cot_moves:
        copy.start()
    turns = list(range(1, half)) + [0]
    order = [lax.rem(high + k, half) * 2 + 1 - low for k in turns]
    order += [lax.rem(high + k, half) * 2 + low for k in turns]
    hid_moves = []
    for i, node in enumerate(order):
        moves = [
            remote(
                piece(hid, node, peer["rep"]), hid_in.at[node, rep], hs.at[k, i], hr.at[k, i], peer
            )
            for k, peer in enumerate(rep_peers)
        ]
        moves.append(
            pltpu.make_async_copy(piece(hid, node, rep), hid_in.at[node, rep], hid_own.at[i])
        )
        for copy in moves:
            copy.start()
        hid_moves.append(moves)

    for copy in cot_moves:
        copy.wait()
    group_cot = cot_in[...].reshape(group_tokens, key_width)
    shape = (key_width, key_width)
    parity = lax.broadcasted_iota(jnp.int32, shape, 0) & lax.broadcasted_iota(jnp.int32, shape, 1)
    for shift in (8, 4, 2, 1):
        parity = parity ^ (parity >> shift)
    had = (1 - 2 * (parity & 1)).astype(f32).astype(rot.dtype)
    for a in range(2):
        flipped = (group_cot.astype(f32) * table[a : a + 1, :]).astype(rot.dtype)
        rot[:, a * key_width : (a + 1) * key_width] = (
            jnp.dot(flipped, had, preferred_element_type=f32) * scale
        ).astype(rot.dtype)
    acc[...] = jnp.zeros_like(acc)

    def make_term(i):
        for copy in hid_moves[i]:
            copy.wait()
        chunk = hid_in[order[i]].reshape(group_tokens, columns)
        product = lax.dot_general(
            chunk, rot[...], (((0,), (0,)), ((), ())), preferred_element_type=f32
        ).reshape(columns // (2 * PAIR_GAP), 2, PAIR_GAP, 2 * key_width)
        first = product[:, 0, :, :key_width].reshape(columns // 2, key_width)
        second = product[:, 1, :, key_width:].reshape(columns // 2, key_width)
        term[i, :, :key_width] = (first + second).astype(term.dtype)
        term[i, :, key_width:] = (first - second).astype(term.dtype)

    swaps = []
    stays = []

    def use_weights(count, node):
        block = sec_in[node]
        rows = lax.dot_general(
            cot_in[...].reshape(group_tokens, key_width), block, (((1,), (1,)), ((), ())),
            preferred_element_type=f32,
        )
        grad[node] = rows.astype(grad.dtype).reshape(reps, tok_rows, columns)
        for k, peer in enumerate(rep_peers):
            copy = remote(
                grad.at[node, peer["rep"]], piece(grad_out, node, rep),
                gs.at[k, count], gr.at[k, count], peer,
            )
            copy.start()
            swaps.append(copy)
        copy = pltpu.make_async_copy(
            grad.at[node, rep], piece(grad_out, node, rep), grad_own.at[count]
        )
        copy.start()
        stays.append(copy)
        chunk = hid_in[node].reshape(group_tokens, columns)
        acc[...] += jnp.dot(chunk, block, preferred_element_type=f32)

    pairs = []
    for i in range(half):
        make_term(i)
        pairs.append(remote(term.at[i], from_pair.at[i], ps.at[i], pr.at[i], partner))
        pairs[-1].start()
        if i:
            weights.forward(i)
    weights.local.wait()
    onward = []
    for j, k in enumerate(turns):
        make_term(half + j)
        pairs[j].wait_recv()
        total = term[half + j].astype(f32) + from_pair[j].astype(f32)
        if k:
            to_same[j] = total.astype(to_same.dtype)
            onward.append(remote(to_same.at[j], from_same.at[j], zs.at[j], zr.at[j], same[k - 1]))
            onward[-1].start()
        else:
            coded[...] = total
        use_weights(j, order[half + j])
    for j in range(half):
        weights.second[j].wait_recv()
        use_weights(half + j, lax.rem(high + half - j, half) * 2 + 1 - low)
    part[...] = acc[...].astype(part.dtype).reshape(part.shape)
    key_moves = [
        remote(part.at[peer["rep"]], key_in.at[k], ks.at[k], kr.at[k], peer)
        for k, peer in enumerate(rep_peers)
    ]
    for copy in key_moves:
        copy.start()
    for j, copy in enumerate(onward):
        copy.wait_recv()
        coded[...] += from_same[j].astype(f32)
    total = part[rep].astype(f32)
    for k, copy in enumerate(key_moves):
        copy.wait_recv()
        total = total + key_in[k].astype(f32)
    keys[...] = total.astype(keys.dtype)
    for copy in swaps:
        copy.wait()
    for copy in stays:
        copy.wait()
    for copy in weights.first + weights.second + pairs + onward + key_moves:
        copy.wait_send()


def step(nodes, reps, aligned, scale, hid, cot, sec, table):
    dma = pltpu.SemaphoreType.DMA
    half = nodes // 2
    columns = sec.shape[0] // reps
    tok_rows, key_width = cot.shape
    group_tokens = reps * tok_rows
    block = (columns // 2, 2 * key_width)
    bf16 = jnp.bfloat16
    return pl.pallas_call(
        functools.partial(step_kernel, nodes, reps, aligned, scale),
        out_shape=(
            jax.ShapeDtypeStruct(block, jnp.float32),
            jax.ShapeDtypeStruct(cot.shape, bf16),
            jax.ShapeDtypeStruct(hid.shape, bf16),
        ),
        in_specs=[ANY, ANY, ANY, VMEM],
        out_specs=(VMEM,) * 3,
        scratch_shapes=[
            pltpu.VMEM((nodes, reps, tok_rows, columns), bf16),
            pltpu.VMEM((reps, tok_rows, key_width), bf16),
            pltpu.VMEM((nodes, columns, key_width), bf16),
            pltpu.VMEM((group_tokens, 2 * key_width), bf16),
            pltpu.VMEM((nodes,) + block, bf16),
            pltpu.VMEM((nodes, reps, tok_rows, columns), bf16),
            pltpu.VMEM((group_tokens, key_width), jnp.float32),
            pltpu.VMEM((reps, tok_rows, key_width), bf16),
            pltpu.VMEM((half,) + block, bf16),
            pltpu.VMEM((half - 1,) + block, bf16),
            pltpu.VMEM((half - 1,) + block, bf16),
            pltpu.VMEM((reps - 1, tok_rows, key_width), bf16),
        ]
        + [dma((reps - 1,))] * 2
        + [dma((reps - 1, nodes))] * 2
        + [dma((2, half))] * 2
        + [dma((half,))] * 2
        + [dma((half - 1,))] * 2
        + [dma((reps - 1, nodes))] * 2
        + [dma((reps - 1,))] * 2
        + [dma((1,)), dma((nodes,)), dma((1,)), dma((nodes,))],
        compiler_params=pltpu.CompilerParams(collective_id=0, has_side_effects=True),
    )(hid, cot, sec, table)


def spread_kernel(reps, src, out, send, recv, local):
    partner, same = pair_peers("rep", reps)
    greet([partner] + same)
    rows = PairGather("rep", reps, src, out, local.at[0], send, recv)
    rows.start()
    for k in range(1, reps // 2):
        rows.forward(k)
    rows.finish()


def spread(reps, rows):
    dma = pltpu.SemaphoreType.DMA
    return pl.pallas_call(
        functools.partial(spread_kernel, reps),
        out_shape=jax.ShapeDtypeStruct((reps,) + rows.shape, rows.dtype),
        in_specs=[VMEM],
        out_specs=VMEM,
        scratch_shapes=[dma((2, reps // 2))] * 2 + [dma((1,))],
        compiler_params=pltpu.CompilerParams(collective_id=1, has_side_effects=True),
    )(rows)


def shards(tokens, norm_gain, key_cotangent, secondary, master, moment_first, moment_second, signs):
    tok_rows, model_width = tokens.shape
    key_width = key_cotangent.shape[1]
    nodes = lax.axis_size("node")
    reps = lax.axis_size("rep")
    all_tokens = tok_rows * nodes * reps
    master_rows = master.shape[0]
    had_table = sylvester(key_width)
    sign_rows = (1 - 2 * signs).astype(jnp.float32).reshape(2, key_width)
    floats = tokens.astype(jnp.float32)
    inverse = lax.rsqrt(jnp.mean(floats * floats, axis=-1, keepdims=True) + norm_eps)
    normed = floats * inverse
    hidden = (normed * norm_gain).astype(jnp.bfloat16)
    aligned = master_rows % 128 == 0
    if not aligned:
        hidden = hidden.reshape(tok_rows, nodes * reps, master_rows).transpose(1, 0, 2)
    rot_scale = 1.0 / (math.sqrt(2 * key_width) * all_tokens)
    coded, keys, hidden_grad = step(
        nodes, reps, aligned, rot_scale, hidden, key_cotangent, secondary,
        sign_rows,
    )
    if not aligned:
        hidden_grad = hidden_grad.transpose(1, 0, 2).reshape(tok_rows, model_width)
    hidden_grad = hidden_grad.astype(jnp.float32)
    new_first = beta_first * moment_first + (1.0 - beta_first) * coded
    new_second = beta_second * moment_second + (1.0 - beta_second) * coded * coded
    first_hat = new_first / (1.0 - beta_first**adam_steps)
    second_hat = new_second / (1.0 - beta_second**adam_steps)
    ratio = first_hat / (jnp.sqrt(second_hat) + adam_eps)
    lower = ratio[:, :key_width]
    upper = ratio[:, key_width:]
    norm_root = math.sqrt(2 * key_width)
    row_even = (
        jnp.dot(lower + upper, had_table, precision=lax.Precision.HIGHEST)
        / norm_root
        * sign_rows[0]
    )
    row_odd = (
        jnp.dot(lower - upper, had_table, precision=lax.Precision.HIGHEST)
        / norm_root
        * sign_rows[1]
    )
    groups = master_rows // (2 * PAIR_GAP)
    update = jnp.stack(
        [
            row_even.reshape(groups, PAIR_GAP, key_width),
            row_odd.reshape(groups, PAIR_GAP, key_width),
        ],
        axis=1,
    ).reshape(master_rows, key_width)
    new_master = master - learn_rate * (update + weight_decay * master)
    new_secondary = spread(reps, new_master.astype(jnp.bfloat16)).reshape(
        reps * master_rows, key_width
    )
    scaled = hidden_grad * norm_gain
    token_grad = (
        inverse * (scaled - normed * jnp.mean(scaled * normed, axis=-1, keepdims=True))
    ).astype(jnp.bfloat16)
    return (keys, token_grad, new_master, new_first, new_second, new_secondary)


def solution(mesh):
    return jax.shard_map(
        shards,
        mesh=mesh,
        in_specs=(
            P(("node", "rep"), None),
            P(),
            P(("node", "rep"), None),
            P("node", None),
            P(("node", "rep"), None),
            P(("node", "rep"), None),
            P(("node", "rep"), None),
            P(),
        ),
        out_specs=(
            P(("node", "rep"), None),
            P(("node", "rep"), None),
            P(("node", "rep"), None),
            P(("node", "rep"), None),
            P(("node", "rep"), None),
            P("node", None),
        ),
        check_vma=False,
    )
```

profile of v0, /device:TPU:0, one launch (start us, length us, event | category | flops | bytes accessed | tf_op | source)
XLA Modules:
  0.0 109.5 jit_solution(6725660948402054318)
XLA Ops:
  0.6 0.0 copy-start
  0.6 0.0 copy-start.6
  0.7 2.2 %fusion.8 = f32[128]{0:T(128)S(1)} fusion(bf16[128,8192]{1,0:T(8,128)(2,1)} %param.8), kind=kLoop, calls=%fused_computation.10 | loop fusion | flops 3145600 | bytes 2097664 | tf_op jit(solution)/shard_map/reduce_sum | solution.py:332
  2.9 0.7 subtract_convert_fusion
  3.6 0.6 reshape.164.table
  4.2 0.0 copy-done
  4.2 0.0 copy-done.6
  4.2 1.9 %fusion.3.hid = bf16[128,8192]{1,0:T(8,128)(2,1)} fusion(bf16[128,8192]{1,0:T(8,128)(2,1)S(1)} %copy-done, f32[8192]{0:T(1024)S(1)} %copy-done.6, f32[128]{0:T(128)S(1)} %add_rsqrt_fusion), kind=kLoop, calls=%fused_computation.5 | loop fusion | flops 4194304 | bytes 4227584 | tf_op jit(solution)/shard_map/convert_element_type | solution.py:334
  6.1 76.1 %shard_map.127 = (f32[128,1024]{1,0:T(8,128)}, bf16[128,512]{1,0:T(8,128)(2,1)}, bf16[128,8192]{1,0:T(8,128)(2,1)}) custom-call(bf16[128,8192]{1,0:T(8,128)(2,1)} %fusion.3.hid, bf16[128,512]{1,0:T(8,128)(2,1)} %cot.1, bf16[1024,512]{1,0:T(8,128)(2,1)} %sec.1, f32[2,512]{1,0:T(2,128)} %reshape.164.table), custom_call_target="tpu_custom_call" | custom-call | tf_op jit(solution)/shard_map/pallas_call | solution.py:265
  82.2 0.0 copy-start.1
  82.3 2.7 %fusion.4 = f32[128]{0:T(128)S(1)} fusion(bf16[128,8192]{1,0:T(8,128)(2,1)S(1)} %copy-done, bf16[128,8192]{1,0:T(8,128)(2,1)} %get-tuple-element.10, f32[8192]{0:T(1024)S(1)} %copy-done.6, f32[128]{0:T(128)S(1)} %add_rsqrt_fusion), kind=kLoop, calls=%fused_computation.6 | loop fusion | flops 6291328 | bytes 4228096 | tf_op jit(solution)/shard_map/reduce_sum | solution.py:378
  85.0 0.0 copy-start.3
  85.0 0.0 copy-start.4
  85.0 0.0 copy-start.5
  85.0 2.4 %fusion.7 = bf16[128,8192]{1,0:T(8,128)(2,1)} fusion(bf16[128,8192]{1,0:T(8,128)(2,1)S(1)} %copy-done, bf16[128,8192]{1,0:T(8,128)(2,1)S(1)} %copy-done.1, f32[128]{0:T(128)S(1)} %broadcast_multiply_fusion, f32[8192]{0:T(1024)S(1)} %copy-done.6, f32[128]{0:T(128)S(1)} %add_rsqrt_fusion), kind=kLoop, calls=%fused_computation.9 | loop fusion | flops 8388608 | bytes 6325248 | tf_op jit(solution)/shard_map/convert_element_type | solution.py:379
  87.4 0.0 copy-done.3
  87.4 1.3 %add_divide_fusion = (f32[128,1024]{1,0:T(8,128)S(1)}, f32[128,1024]{1,0:T(8,128)}, f32[128,1024]{1,0:T(8,128)}) fusion(f32[128,1024]{1,0:T(8,128)S(1)} %copy-done.5, f32[128,1024]{1,0:T(8,128)S(1)} %copy-done.3, f32[128,1024]{1,0:T(8,128)S(1)} %copy-done.4), kind=kLoop, calls=%fused_computation.27 | loop fusion | flops 1441792 | bytes 3145728 | tf_op jit(solution)/shard_map/div | solution.py:350
  88.7 1.9 %convolution_multiply_fusion.1 = f32[128,512]{1,0:T(8,128)S(1)} fusion(s32[512]{0:T(512)S(1)} %get-tuple-element.19, s32[512]{0:T(512)S(1)} %get-tuple-element.20, s32[512]{0:T(512)S(1)} %get-tuple-element.21, s32[512]{0:T(512)S(1)} %get-tuple-element.22, s32[512]{0:T(512)S(1)} %get-tuple-element.23, s32[512]{0:T(512)S(1)} %get-tuple-element.24, ...), kind=kOutput, calls=%fused_computation.16 | convolution fusion | flops 410910720 | bytes 825344 | tf_op jit(solution)/shard_map/dot_general | solution.py:355
  90.6 0.0 copy-start.2
  90.6 1.9 %convolution_multiply_fusion = f32[128,512]{1,0:T(8,128)S(1)} fusion(s32[512]{0:T(512)S(1)} %get-tuple-element.19, s32[512]{0:T(512)S(1)} %get-tuple-element.20, s32[512]{0:T(512)S(1)} %get-tuple-element.21, s32[512]{0:T(512)S(1)} %get-tuple-element.22, s32[512]{0:T(512)S(1)} %get-tuple-element.23, s32[512]{0:T(512)S(1)} %get-tuple-element.24, ...), kind=kOutput, calls=%fused_computation.15 | convolution fusion | flops 410910720 | bytes 825344 | tf_op jit(solution)/shard_map/dot_general | solution.py:360
  92.6 1.0 fusion.30
  93.6 13.0 %shard_map.128 = bf16[4,256,512]{2,1,0:T(8,128)(2,1)} custom-call(bf16[256,512]{1,0:T(8,128)(2,1)} %get-tuple-element.12.src), custom_call_target="tpu_custom_call" | custom-call | tf_op jit(solution)/shard_map/pallas_call | solution.py:312
  106.6 0.7 copy.18
  107.3 2.3 %copy.19 = bf16[1024,512]{1,0:T(8,128)(2,1)} copy(bf16[1024,512]{1,0:T(8,128)(2,1)} %bitcast.14) | data formatting | bytes 2097152
  (15 shorter events, 0.1 us)
Async XLA Ops:
  0.6 3.6 %copy-start = (bf16[128,8192]{1,0:T(8,128)(2,1)S(1)}, bf16[128,8192]{1,0:T(8,128)(2,1)}, u32[]{:S(2)}) copy-start(bf16[128,8192]{1,0:T(8,128)(2,1)} %param.8) | copy-start | bytes 6291460
  0.6 3.6 %copy-start.6 = (f32[8192]{0:T(1024)S(1)}, f32[8192]{0:T(1024)}, u32[]{:S(2)}) copy-start(f32[8192]{0:T(1024)} %param.9) | copy-start | bytes 98308
  82.2 2.7 %copy-start.1 = (bf16[128,8192]{1,0:T(8,128)(2,1)S(1)}, bf16[128,8192]{1,0:T(8,128)(2,1)}, u32[]{:S(2)}) copy-start(bf16[128,8192]{1,0:T(8,128)(2,1)} %get-tuple-element.10) | copy-start | bytes 6291460
  85.0 2.4 %copy-start.3 = (f32[128,1024]{1,0:T(8,128)S(1)}, f32[128,1024]{1,0:T(8,128)}, u32[]{:S(2)}) copy-start(f32[128,1024]{1,0:T(8,128)} %param.13) | copy-start | bytes 1572868
  85.0 2.4 %copy-start.4 = (f32[128,1024]{1,0:T(8,128)S(1)}, f32[128,1024]{1,0:T(8,128)}, u32[]{:S(2)}) copy-start(f32[128,1024]{1,0:T(8,128)} %param.14) | copy-start | bytes 1572868
  85.0 2.4 %copy-start.5 = (f32[128,1024]{1,0:T(8,128)S(1)}, f32[128,1024]{1,0:T(8,128)}, u32[]{:S(2)}) copy-start(f32[128,1024]{1,0:T(8,128)} %get-tuple-element.11) | copy-start | bytes 1572868
  90.6 2.0 %copy-start.2 = (f32[256,512]{1,0:T(8,128)S(1)}, f32[256,512]{1,0:T(8,128)}, u32[]{:S(2)}) copy-start(f32[256,512]{1,0:T(8,128)} %param.12) | copy-start | bytes 1572868
  92.5 14.1 %copy-start.7 = (bf16[128,512]{1,0:T(8,128)(2,1)S(1)}, bf16[128,512]{1,0:T(8,128)(2,1)}, u32[]{:S(2)}) copy-start(bf16[128,512]{1,0:T(8,128)(2,1)} %get-tuple-element.33) | copy-start | bytes 393220
where the time goes:
time: 110 us
  Pallas kernels  89.1 us (81%)
  other arithmetic  12.3 us (11%)
  matrix products  3.78 us (3%)
  local copies, waits for them, and re-layouts  3.56 us (3%)
    pallas_call x1, Pallas kernels, step(): pl.pallas_call(functools.partial(step_kernel, nodes, reps, aligned, scale...  76.1 us
    pallas_call x1, Pallas kernels, spread(): pl.pallas_call(functools.partial(spread_kernel, reps), out_shape=jax.Shap...  13 us
    unnamed x18, local copies, waits for them, and re-layouts  2.96 us
    reduce_sum x1, other arithmetic, shards(): jnp.mean(scaled * normed, axis=-1, keepdims=True)  2.7 us
    convert_element_type x1, other arithmetic, shards(): token_grad = (inverse * (scaled - normed * jnp.mean(scaled * normed, axis...  2.39 us
    reduce_sum x1, other arithmetic, shards(): jnp.mean(floats * floats, axis=-1, keepdims=True) + norm_eps  2.22 us

commit v1 on v0

--- a/solution.py
+++ b/solution.py
@@ -20,6 +20,7 @@
 weight_decay = 0.1
 
 ANY = pl.BlockSpec(memory_space=pl.ANY)
+HBM = pl.BlockSpec(memory_space=pltpu.HBM)
 VMEM = pl.BlockSpec(memory_space=pltpu.VMEM)
 
 
@@ -319,6 +320,450 @@
     )(rows)
 
 
+def flip(index, bits):
+    for bit in (1, 2, 4):
+        if bits & bit:
+            index = index + bit * (1 - 2 * lax.rem(lax.div(index, bit), 2))
+    return index
+
+
+def fused_kernel(
+    nodes, reps, scale,
+    tok, gain, cot, sec, master, first, second, signs,
+    keys_out, grad_out, master_out, first_out, second_out, sec_out,
+    x_in, hid, hid_in, cot_in, sec_in, sec_own, rot, had, term, total, from_pair,
+    to_near, from_near, to_far, from_far, grad, grad_in, acc, inv,
+    part, part_in, cross, cross_in, master_in, first_in, second_in,
+    xl, ll, cs, cr, hs, hr, ws, wr, ps, pr, zs, zr, gs, gr, ks, kr, ss, sr,
+):
+    f32, bf16 = jnp.float32, jnp.bfloat16
+    rep = lax.axis_index("rep")
+    me = lax.axis_index("node")
+    pieces, tok_rows, columns = x_in.shape
+    key_width = cot_in.shape[2]
+    group_tokens = reps * tok_rows
+    half = columns // 2
+    rep_kinds = (2, 3, 1)
+    rep_peer = {k: {"rep": flip(rep, k)} for k in rep_kinds}
+    node_peer = {k: {"node": flip(me, k)} for k in (1, 2, 4)}
+
+    loads = [
+        pltpu.make_async_copy(tok.at[:, pl.ds(columns * i, columns)], x_in.at[i], xl.at[i])
+        for i in range(pieces)
+    ]
+    own_cot = pltpu.make_async_copy(cot, cot_in.at[rep], ll.at[0])
+    own_sec = pltpu.make_async_copy(sec, sec_own, ll.at[1])
+    state = [
+        pltpu.make_async_copy(master, master_in, ll.at[2]),
+        pltpu.make_async_copy(first, first_in, ll.at[3]),
+        pltpu.make_async_copy(second, second_in, ll.at[4]),
+    ]
+    for copy in loads + [own_cot, own_sec] + state:
+        copy.start()
+    greet([rep_peer[k] for k in rep_kinds] + [node_peer[k] for k in (1, 2, 4)])
+
+    sent = []
+
+    def go(copy):
+        copy.start()
+        sent.append(copy)
+        return copy
+
+    quarter = sec.at[pl.ds(pl.multiple_of(rep * columns, columns), columns)]
+    slots = {}
+
+    def weight(source, via):
+        slot = len(slots)
+        src = sec_in.at[flip(me, source)] if source else quarter
+        copy = remote(src, sec_in.at[flip(me, source)], ws.at[slot], wr.at[slot], node_peer[via])
+        slots[source ^ via] = go(copy)
+
+    held = set()
+
+    def arrived(bits):
+        if bits not in held:
+            held.add(bits)
+            slots[bits].wait_recv()
+
+    weight(0, 4)
+    weight(0, 1)
+    weight(0, 2)
+    cot_moves = {
+        2: go(remote(cot, cot_in.at[rep], cs.at[0], cr.at[0], rep_peer[2])),
+        1: go(remote(cot, cot_in.at[rep], cs.at[1], cr.at[1], rep_peer[1])),
+    }
+
+    for copy in loads:
+        copy.wait()
+
+    def squares(i, running):
+        x = x_in[i].astype(f32)
+        x = x * x
+        for lane in range(0, columns, 128):
+            running = running + x[:, lane : lane + 128]
+        return running
+
+    squared = lax.fori_loop(0, pieces, squares, jnp.zeros((tok_rows, 128), f32))
+    mean = jnp.sum(squared, axis=-1, keepdims=True) * (1.0 / (pieces * columns))
+    inv[...] = jnp.broadcast_to(lax.rsqrt(mean + norm_eps), inv.shape)
+
+    order = [7, 3, 5, 1, 6, 2, 4, 0]
+    hid_moves = []
+    for i, bits in enumerate(order):
+        node = flip(me, bits)
+        moves = []
+        for k in rep_kinds + (0,):
+            owner = flip(rep, k)
+            index = node * reps + owner
+            value = (x_in[index].astype(f32) * inv[...] * gain[index]).astype(bf16)
+            if k:
+                hid[node, owner] = value
+                moves.append(
+                    go(
+                        remote(
+                            hid.at[node, owner], hid_in.at[node, rep],
+                            hs.at[k - 1, i], hr.at[k - 1, i], rep_peer[k],
+                        )
+                    )
+                )
+            else:
+                hid_in[node, rep] = value
+        hid_moves.append(moves)
+
+    shape = (key_width, key_width)
+    parity = lax.broadcasted_iota(jnp.int32, shape, 0) & lax.broadcasted_iota(jnp.int32, shape, 1)
+    for shift in (8, 4, 2, 1):
+        parity = parity ^ (parity >> shift)
+    had[...] = (1 - 2 * (parity & 1)).astype(f32).astype(bf16)
+    chunks = key_width // 128
+    sign_row = []
+    for a in range(2):
+        bits = [signs[a * chunks + c : a * chunks + c + 1, :] for c in range(chunks)]
+        sign_row.append((1 - 2 * jnp.concatenate(bits, axis=1)).astype(f32))
+
+    cot_moves[2].wait_recv()
+    across = cot_in.at[flip(rep, 2)]
+    cot_moves[3] = go(remote(across, across, cs.at[2], cr.at[2], rep_peer[1]))
+    own_cot.wait()
+    cot_moves[1].wait_recv()
+    cot_moves[3].wait_recv()
+    for a in range(2):
+        flipped = (cot_in[...].reshape(group_tokens, key_width).astype(f32) * sign_row[a]).astype(bf16)
+        rot[:, a * key_width : (a + 1) * key_width] = (
+            jnp.dot(flipped, had[...], preferred_element_type=f32) * scale
+        ).astype(bf16)
+
+    def make_term(i):
+        for copy in hid_moves[i]:
+            copy.wait_recv()
+        chunk = hid_in[flip(me, order[i])].reshape(group_tokens, columns)
+        product = lax.dot_general(
+            chunk, rot[...], (((0,), (0,)), ((), ())), preferred_element_type=f32
+        ).reshape(columns // (2 * PAIR_GAP), 2, PAIR_GAP, 2 * key_width)
+        upper = product[:, 0, :, :key_width].reshape(half, key_width)
+        lower = product[:, 1, :, key_width:].reshape(half, key_width)
+        return upper + lower, upper - lower
+
+    def halves(ref):
+        return ref[:, :key_width].astype(f32), ref[:, key_width:].astype(f32)
+
+    def put(ref, pair):
+        ref[:, :key_width] = pair[0].astype(ref.dtype)
+        ref[:, key_width:] = pair[1].astype(ref.dtype)
+
+    def plus(a, b):
+        return a[0] + b[0], a[1] + b[1]
+
+    grad_moves = {}
+
+    def local_grads():
+        own_sec.wait()
+        for k in range(reps):
+            block = sec_own[pl.ds(k * columns, columns)]
+            grad_in[me * reps + k] = lax.dot_general(
+                cot_in[rep], block, (((1,), (1,)), ((), ())), preferred_element_type=f32
+            ).astype(bf16)
+        grad_moves[0] = []
+
+    def use_grads(bits):
+        arrived(bits)
+        node = flip(me, bits)
+        rows = lax.dot_general(
+            cot_in[...].reshape(group_tokens, key_width), sec_in[node], (((1,), (1,)), ((), ())),
+            preferred_element_type=f32,
+        )
+        grad[node] = rows.astype(bf16).reshape(reps, tok_rows, columns)
+        slot = len(grad_moves)
+        grad_moves[bits] = [
+            go(
+                remote(
+                    grad.at[node, flip(rep, k)], grad_in.at[node * reps + rep],
+                    gs.at[k - 1, slot], gr.at[k - 1, slot], rep_peer[k],
+                )
+            )
+            for k in rep_kinds
+        ]
+        grad_in[node * reps + rep] = grad[node, rep]
+
+    def use_keys(bits, start=False):
+        node = flip(me, bits)
+        block = sec_in[node] if bits else sec_own[pl.ds(pl.multiple_of(rep * columns, columns), columns)]
+        product = jnp.dot(
+            hid_in[node].reshape(group_tokens, columns), block, preferred_element_type=f32
+        )
+        if start:
+            acc[...] = product
+        else:
+            acc[...] += product
+
+    pairs = []
+    for i in range(4):
+        put(term.at[i], make_term(i))
+        pairs.append(go(remote(term.at[i], from_pair.at[i], ps.at[i], pr.at[i], node_peer[1])))
+        if i == 0:
+            arrived(4)
+            weight(4, 2)
+            local_grads()
+        if i == 1:
+            arrived(1)
+            weight(1, 2)
+            use_grads(1)
+        if i == 2:
+            use_grads(4)
+        if i == 3:
+            weight(4, 1)
+            use_grads(2)
+            use_keys(1, True)
+    near = []
+    for j in range(2):
+        value = make_term(4 + j)
+        pairs[j].wait_recv()
+        put(to_near.at[j], plus(value, halves(from_pair.at[j])))
+        near.append(go(remote(to_near.at[j], from_near.at[j], zs.at[j], zr.at[j], node_peer[2])))
+        if j == 0:
+            arrived(6)
+            weight(6, 1)
+            use_grads(6)
+            use_keys(6)
+        if j == 1:
+            use_keys(2)
+    put(total.at[0], make_term(6))
+    use_keys(4)
+    use_grads(3)
+    use_keys(3)
+    put(total.at[1], make_term(7))
+    use_keys(0)
+    pairs[2].wait_recv()
+    near[0].wait_recv()
+    put(
+        to_far,
+        plus(halves(total.at[0]), plus(halves(from_pair.at[2]), halves(from_near.at[0]))),
+    )
+    far = go(remote(to_far, from_far, zs.at[2], zr.at[2], node_peer[4]))
+    pairs[3].wait_recv()
+    near[1].wait_recv()
+    put(
+        total.at[1],
+        plus(halves(total.at[1]), plus(halves(from_pair.at[3]), halves(from_near.at[1]))),
+    )
+    use_grads(5)
+    use_keys(5)
+
+    for copy in state:
+        copy.wait()
+    far.wait_recv()
+    coded = total[1] + from_far[...].astype(f32)
+    new_first = beta_first * first_in[...] + (1.0 - beta_first) * coded
+    new_second = beta_second * second_in[...] + (1.0 - beta_second) * coded * coded
+    first_out[...] = new_first
+    second_out[...] = new_second
+    first_hat = new_first / (1.0 - beta_first**adam_steps)
+    second_hat = new_second / (1.0 - beta_second**adam_steps)
+    ratio = first_hat / (jnp.sqrt(second_hat) + adam_eps)
+    norm_root = math.sqrt(2 * key_width)
+    rows = []
+    for a in range(2):
+        if a:
+            mixed = ratio[:, :key_width] - ratio[:, key_width:]
+        else:
+            mixed = ratio[:, :key_width] + ratio[:, key_width:]
+        turned = jnp.zeros_like(mixed)
+        for _ in range(3):
+            high = mixed.astype(bf16)
+            mixed = mixed - high.astype(f32)
+            turned = turned + jnp.dot(high, had[...], preferred_element_type=f32)
+        rows.append(
+            (turned * (1.0 / norm_root) * sign_row[a]).reshape(
+                half // PAIR_GAP, 1, PAIR_GAP, key_width
+            )
+        )
+    update = jnp.concatenate(rows, axis=1).reshape(columns, key_width)
+    new_master = master_in[...] - learn_rate * (update + weight_decay * master_in[...])
+    master_out[...] = new_master
+    sec_out[rep] = new_master.astype(bf16)
+    mine = sec_out.at[rep]
+    spread_moves = {
+        k: go(remote(mine, mine, ss.at[k - 1], sr.at[k - 1], rep_peer[k])) for k in (2, 1)
+    }
+
+    use_grads(7)
+    use_keys(7)
+    for i, k in enumerate((3, 1)):
+        owner = flip(rep, k)
+        part[i] = acc[pl.ds(pl.multiple_of(owner * tok_rows, tok_rows), tok_rows)].astype(bf16)
+    part_move = go(remote(part, part_in, ks.at[0], kr.at[0], rep_peer[1]))
+    part_move.wait_recv()
+    away = flip(rep, 2)
+    cross[...] = (
+        acc[pl.ds(pl.multiple_of(away * tok_rows, tok_rows), tok_rows)] + part_in[0].astype(f32)
+    ).astype(bf16)
+    cross_move = go(remote(cross, cross_in, ks.at[1], kr.at[1], rep_peer[2]))
+
+    def overlap(node):
+        def add(k, running):
+            index = node * reps + k
+            value = grad_in[index].astype(f32) * gain[index] * x_in[index].astype(f32)
+            for lane in range(0, columns, 128):
+                running = running + value[:, lane : lane + 128]
+            return running
+
+        return add
+
+    running = jnp.zeros((tok_rows, 128), f32)
+    for bits, moves in grad_moves.items():
+        for copy in moves:
+            copy.wait_recv()
+        running = lax.fori_loop(0, reps, overlap(flip(me, bits)), running)
+    against = jnp.sum(running, axis=-1, keepdims=True) * (1.0 / (pieces * columns))
+    one = inv[:, :1]
+    factor = jnp.broadcast_to(one * one * one * against, (tok_rows, columns))
+
+    def finish(i, carry):
+        scaled = grad_in[i].astype(f32) * gain[i]
+        grad_out[i] = (inv[...] * scaled - x_in[i].astype(f32) * factor).astype(bf16)
+        return carry
+
+    lax.fori_loop(0, pieces, finish, 0)
+
+    spread_moves[2].wait_recv()
+    across = sec_out.at[flip(rep, 2)]
+    spread_moves[3] = go(remote(across, across, ss.at[2], sr.at[2], rep_peer[1]))
+    cross_move.wait_recv()
+    keys_out[...] = (
+        acc[pl.ds(pl.multiple_of(rep * tok_rows, tok_rows), tok_rows)]
+        + part_in[1].astype(f32)
+        + cross_in[...].astype(f32)
+    ).astype(keys_out.dtype)
+    spread_moves[1].wait_recv()
+    spread_moves[3].wait_recv()
+    for copy in sent:
+        copy.wait_send()
+
+
+def store_kernel(keys, grad, master, first, second, sec, *refs):
+    keys_out, grad_out, master_out, first_out, second_out, sec_out, sems = refs
+    pieces, _, columns = grad.shape
+    rows = sec.shape[1]
+    moves = [
+        pltpu.make_async_copy(grad.at[i], grad_out.at[:, pl.ds(columns * i, columns)], sems.at[i])
+        for i in range(pieces)
+    ]
+    pairs = [(keys, keys_out), (master, master_out), (first, first_out), (second, second_out)]
+    pairs += [(sec.at[i], sec_out.at[pl.ds(rows * i, rows)]) for i in range(sec.shape[0])]
+    for i, (src, dst) in enumerate(pairs):
+        moves.append(pltpu.make_async_copy(src, dst, sems.at[pieces + i]))
+    for copy in moves:
+        copy.start()
+    for copy in moves:
+        copy.wait()
+
+
+def fused(nodes, reps, scale, tokens, gain, cot, sec, master, first, second, signs):
+    dma = pltpu.SemaphoreType.DMA
+    f32, bf16 = jnp.float32, jnp.bfloat16
+    tok_rows, model_width = tokens.shape
+    key_width = cot.shape[1]
+    columns = master.shape[0]
+    pieces = model_width // columns
+    block = first.shape
+    group_tokens = reps * tok_rows
+    vmem = pltpu.VMEM
+    far = functools.partial(pltpu.with_memory_space_constraint, memory_space=pltpu.HBM)
+    results = pl.pallas_call(
+        functools.partial(fused_kernel, nodes, reps, scale),
+        out_shape=(
+            vmem(cot.shape, bf16),
+            vmem((pieces, tok_rows, columns), bf16),
+            vmem(master.shape, f32),
+            vmem(block, f32),
+            vmem(block, f32),
+            vmem((reps,) + master.shape, bf16),
+        ),
+        in_specs=[HBM, VMEM, HBM, HBM, HBM, HBM, HBM, VMEM],
+        out_specs=(VMEM,) * 6,
+        scratch_shapes=[
+            vmem((pieces, tok_rows, columns), bf16),
+            vmem((nodes, reps, tok_rows, columns), bf16),
+            vmem((nodes, reps, tok_rows, columns), bf16),
+            vmem((reps, tok_rows, key_width), bf16),
+            vmem((nodes, columns, key_width), bf16),
+            vmem(sec.shape, bf16),
+            vmem((group_tokens, 2 * key_width), bf16),
+            vmem((key_width, key_width), bf16),
+            vmem((4,) + block, bf16),
+            vmem((2,) + block, f32),
+            vmem((4,) + block, bf16),
+            vmem((2,) + block, bf16),
+            vmem((2,) + block, bf16),
+            vmem(block, bf16),
+            vmem(block, bf16),
+            vmem((nodes, reps, tok_rows, columns), bf16),
+            vmem((pieces, tok_rows, columns), bf16),
+            vmem((group_tokens, key_width), f32),
+            vmem((tok_rows, columns), f32),
+            vmem((2, tok_rows, key_width), bf16),
+            vmem((2, tok_rows, key_width), bf16),
+            vmem((tok_rows, key_width), bf16),
+            vmem((tok_rows, key_width), bf16),
+            vmem(master.shape, f32),
+            vmem(block, f32),
+            vmem(block, f32),
+        ]
+        + [dma((pieces,)), dma((5,))]
+        + [dma((3,))] * 2
+        + [dma((3, nodes))] * 2
+        + [dma((nodes - 1,))] * 2
+        + [dma((4,))] * 2
+        + [dma((3,))] * 2
+        + [dma((3, nodes))] * 2
+        + [dma((2,))] * 2
+        + [dma((3,))] * 2,
+        compiler_params=pltpu.CompilerParams(
+            collective_id=2, has_side_effects=True, vmem_limit_bytes=56 << 20
+        ),
+    )(
+        far(tokens), gain.reshape(pieces, 1, columns), far(cot), far(sec), far(master),
+        far(first), far(second), signs.reshape(-1, 128),
+    )
+    held = [pltpu.with_memory_space_constraint(value, pltpu.VMEM) for value in results]
+    like = jax.ShapeDtypeStruct
+    return pl.pallas_call(
+        store_kernel,
+        out_shape=(
+            like(cot.shape, bf16),
+            like(tokens.shape, bf16),
+            like(master.shape, f32),
+            like(block, f32),
+            like(block, f32),
+            like(sec.shape, bf16),
+        ),
+        in_specs=[VMEM] * 6,
+        out_specs=(ANY,) * 6,
+        scratch_shapes=[dma((pieces + 4 + reps,))],
+        compiler_params=pltpu.CompilerParams(vmem_limit_bytes=1 << 20),
+    )(*held)
+
+
 def shards(tokens, norm_gain, key_cotangent, secondary, master, moment_first, moment_second, signs):
     tok_rows, model_width = tokens.shape
     key_width = key_cotangent.shape[1]
@@ -326,16 +771,21 @@
     reps = lax.axis_size("rep")
     all_tokens = tok_rows * nodes * reps
     master_rows = master.shape[0]
+    rot_scale = 1.0 / (math.sqrt(2 * key_width) * all_tokens)
+    aligned = master_rows % 128 == 0
+    if aligned and (nodes, reps) == (8, 4):
+        return fused(
+            nodes, reps, rot_scale, tokens, norm_gain, key_cotangent, secondary, master,
+            moment_first, moment_second, signs,
+        )
     had_table = sylvester(key_width)
     sign_rows = (1 - 2 * signs).astype(jnp.float32).reshape(2, key_width)
     floats = tokens.astype(jnp.float32)
     inverse = lax.rsqrt(jnp.mean(floats * floats, axis=-1, keepdims=True) + norm_eps)
     normed = floats * inverse
     hidden = (normed * norm_gain).astype(jnp.bfloat16)
-    aligned = master_rows % 128 == 0
     if not aligned:
         hidden = hidden.reshape(tok_rows, nodes * reps, master_rows).transpose(1, 0, 2)
-    rot_scale = 1.0 / (math.sqrt(2 * key_width) * all_tokens)
     coded, keys, hidden_grad = step(
         nodes, reps, aligned, rot_scale, hidden, key_cotangent, secondary,
         sign_rows,

time: 110 us -> 68.4 us (0.62)
  Pallas kernels: 89.1 us -> 67.6 us
  other arithmetic: 12.3 us -> 0 us
  matrix products: 3.78 us -> 0 us
  local copies, waits for them, and re-layouts: 3.56 us -> 0 us
    pallas_call x2, Pallas kernels: 89.1 us -> 67.6 us  [the longest x1 65.1 us: fused(): pl.pallas_call(functools.partial(fused_kernel, nodes, reps, scale), out_s...]
    convert_element_type x4 -> x0, other arithmetic: 5.99 us -> none  [the longest x1 2.39 us: shards(): token_grad = (inverse * (scaled - normed * jnp.mean(scaled * normed, axis...]
    reduce_sum x2 -> x0, other arithmetic: 4.92 us -> none  [the longest x1 2.7 us: shards(): jnp.mean(scaled * normed, axis=-1, keepdims=True)]
    dot_general x2 -> x0, matrix products: 3.78 us -> none  [the longest x1 1.89 us: shards(): jnp.dot(lower - upper, had_table, precision=lax.Precision.HIGHEST)]
    unnamed x18 -> x0, local copies, waits for them, and re-layouts: 2.96 us -> none
    div x2 -> x0, other arithmetic: 1.3 us -> none  [the longest x1 1.29 us: shards(): ratio = first_hat / (jnp.sqrt(second_hat) + adam_eps)]
where the time goes in v1:
time: 68.4 us; the launch traced here: 68.3 us
  Pallas kernels  67.6 us (99%)
    pallas_call x1, Pallas kernels, fused(): pl.pallas_call(functools.partial(fused_kernel, nodes, reps, scale), out_s...  65.1 us
    pallas_call x1, Pallas kernels, fused(): pl.pallas_call(store_kernel, out_shape=(like(cot.shape, bf16), like(token...  2.55 us

profile of v1, /device:TPU:0, one launch (start us, length us, event | category | flops | bytes accessed | tf_op | source)
XLA Modules:
  0.0 68.3 jit_solution(10365382400921424363)
XLA Ops:
  0.6 65.1 %shard_map.127 = (bf16[128,512]{1,0:T(8,128)(2,1)S(1)}, bf16[32,128,256]{2,1,0:T(8,128)(2,1)S(1)}, f32[256,512]{1,0:T(8,128)S(1)}, f32[128,1024]{1,0:T(8,128)S(1...) custom-call(bf16[128,8192]{1,0:T(8,128)(2,1)} %tok.1, f32[32,1,256]{2,1,0:T(1,128)} %bitcast.2, ...), custom_call_target="tpu_custom_call" | custom-call | tf_op jit(solution)/shard_map/pallas_call | solution.py:692
  65.7 2.5 %shard_map.128 = (bf16[128,512]{1,0:T(8,128)(2,1)}, bf16[128,8192]{1,0:T(8,128)(2,1)}, f32[256,512]{1,0:T(8,128)}, f32[128,1024]{1,0:T(8,128)}, f32[128,1024]{1,0:T(8,128)}, /*index=5*/bf16[1024,512]{1,0:T(8,128)(2,1)}) custom-call(bf16[128,512]{1,0:T(8,128)(2,1)S(1)} %get-tuple-element.12.keys, bf16[32,128,256]{2,1,0:T(8,128)(2,1)S(1)} %get-tuple-element.13.grad, ...), custom_call_target="tpu_custom_call" | custom-call | tf_op jit(solution)/shard_map/pallas_call | solution.py:750

commit v2 on v1

--- a/solution.py
+++ b/solution.py
@@ -333,8 +333,8 @@
     keys_out, grad_out, master_out, first_out, second_out, sec_out,
     x_in, hid, hid_in, cot_in, sec_in, sec_own, rot, had, term, total, from_pair,
     to_near, from_near, to_far, from_far, grad, grad_in, acc, inv,
-    part, part_in, cross, cross_in, master_in, first_in, second_in,
-    xl, ll, cs, cr, hs, hr, ws, wr, ps, pr, zs, zr, gs, gr, ks, kr, ss, sr,
+    part, part_in, cross, cross_in, master_in, first_in, second_in, ext,
+    xl, ll, cs, cr, hs, hr, ws, wr, ps, pr, zs, zr, gs, gr, ks, kr, ss, sr, es, er,
 ):
     f32, bf16 = jnp.float32, jnp.bfloat16
     rep = lax.axis_index("rep")
@@ -407,7 +407,8 @@
     mean = jnp.sum(squared, axis=-1, keepdims=True) * (1.0 / (pieces * columns))
     inv[...] = jnp.broadcast_to(lax.rsqrt(mean + norm_eps), inv.shape)
 
-    order = [7, 3, 5, 1, 6, 2, 4, 0]
+    order = [7, 6, 3, 2, 5, 4, 1, 0]
+    place = {bits: i for i, bits in enumerate(order)}
     hid_moves = []
     for i, bits in enumerate(order):
         node = flip(me, bits)
@@ -453,10 +454,10 @@
             jnp.dot(flipped, had[...], preferred_element_type=f32) * scale
         ).astype(bf16)
 
-    def make_term(i):
-        for copy in hid_moves[i]:
+    def make_term(bits):
+        for copy in hid_moves[place[bits]]:
             copy.wait_recv()
-        chunk = hid_in[flip(me, order[i])].reshape(group_tokens, columns)
+        chunk = hid_in[flip(me, bits)].reshape(group_tokens, columns)
         product = lax.dot_general(
             chunk, rot[...], (((0,), (0,)), ((), ())), preferred_element_type=f32
         ).reshape(columns // (2 * PAIR_GAP), 2, PAIR_GAP, 2 * key_width)
@@ -464,15 +465,11 @@
         lower = product[:, 1, :, key_width:].reshape(half, key_width)
         return upper + lower, upper - lower
 
-    def halves(ref):
-        return ref[:, :key_width].astype(f32), ref[:, key_width:].astype(f32)
-
-    def put(ref, pair):
-        ref[:, :key_width] = pair[0].astype(ref.dtype)
-        ref[:, key_width:] = pair[1].astype(ref.dtype)
-
-    def plus(a, b):
-        return a[0] + b[0], a[1] + b[1]
+    def add_up(dst, *parts):
+        value = parts[0].astype(f32)
+        for other in parts[1:]:
+            value = value + other.astype(f32)
+        dst[...] = value.astype(dst.dtype)
 
     grad_moves = {}
 
@@ -516,96 +513,159 @@
         else:
             acc[...] += product
 
-    pairs = []
-    for i in range(4):
-        put(term.at[i], make_term(i))
-        pairs.append(go(remote(term.at[i], from_pair.at[i], ps.at[i], pr.at[i], node_peer[1])))
-        if i == 0:
-            arrived(4)
-            weight(4, 2)
-            local_grads()
-        if i == 1:
-            arrived(1)
-            weight(1, 2)
-            use_grads(1)
-        if i == 2:
-            use_grads(4)
-        if i == 3:
-            weight(4, 1)
-            use_grads(2)
-            use_keys(1, True)
-    near = []
-    for j in range(2):
-        value = make_term(4 + j)
-        pairs[j].wait_recv()
-        put(to_near.at[j], plus(value, halves(from_pair.at[j])))
-        near.append(go(remote(to_near.at[j], from_near.at[j], zs.at[j], zr.at[j], node_peer[2])))
-        if j == 0:
-            arrived(6)
-            weight(6, 1)
-            use_grads(6)
-            use_keys(6)
-        if j == 1:
-            use_keys(2)
-    put(total.at[0], make_term(6))
-    use_keys(4)
+    near_nodes = (2,)
+    extra = {}
+
+    def fetch(e):
+        other = sec.at[pl.ds(pl.multiple_of(flip(rep, 2) * columns, columns), columns)]
+        bits = near_nodes[e]
+        extra[e] = [go(remote(other, ext.at[e, 2], es.at[e, 2], er.at[e, 2], node_peer[bits]))]
+
+    def pass_on(e):
+        node = flip(me, near_nodes[e])
+        arrived(near_nodes[e])
+        extra[e][0].wait_recv()
+        for k, src in ((1, sec_in.at[node]), (3, ext.at[e, 2])):
+            extra[e].append(go(remote(src, ext.at[e, k], es.at[e, k], er.at[e, k], rep_peer[1])))
+
+    def extra_grads(e):
+        node = flip(me, near_nodes[e])
+        for copy in extra[e][1:]:
+            copy.wait_recv()
+        for k in range(4):
+            block = ext[e, k] if k else sec_in[node]
+            grad_in[node * reps + flip(rep, k)] = lax.dot_general(
+                cot_in[rep], block, (((1,), (1,)), ((), ())), preferred_element_type=f32
+            ).astype(bf16)
+        grad_moves[near_nodes[e]] = []
+
+    pair_moves, near_moves, far_moves = {}, {}, {}
+
+    def to_pair(i, bits):
+        upper, lower = make_term(bits)
+        rows = upper.shape[0] // 2
+        for h in range(2):
+            term[i, h, :, :key_width] = upper[h * rows : (h + 1) * rows].astype(bf16)
+            term[i, h, :, key_width:] = lower[h * rows : (h + 1) * rows].astype(bf16)
+            pair_moves[i, h] = go(
+                remote(term.at[i, h], from_pair.at[i, h], ps.at[i, h], pr.at[i, h], node_peer[1])
+            )
+
+    def keep(i, bits):
+        upper, lower = make_term(bits)
+        total[i, :, :key_width] = upper
+        total[i, :, key_width:] = lower
+
+    def mine(i, h):
+        rows = total.shape[1] // 2
+        return total[i, h * rows : (h + 1) * rows]
+
+    def to_neighbour(i, h):
+        pair_moves[i, h].wait_recv()
+        add_up(to_near.at[i, h], mine(i, h), from_pair[i, h])
+        near_moves[i, h] = go(
+            remote(to_near.at[i, h], from_near.at[i, h], zs.at[i, h], zr.at[i, h], node_peer[2])
+        )
+
+    def to_distant(h):
+        pair_moves[2, h].wait_recv()
+        near_moves[0, h].wait_recv()
+        add_up(to_far.at[h], mine(2, h), from_pair[2, h], from_near[0, h])
+        far_moves[h] = go(remote(to_far.at[h], from_far.at[h], zs.at[2, h], zr.at[2, h], node_peer[4]))
+
+    spread_moves = {}
+    norm_root = math.sqrt(2 * key_width)
+    master_half = columns // 2
+
+    def spread_block(owner, h):
+        return sec_out.at[owner, pl.ds(h * master_half, master_half)]
+
+    def finalize(h):
+        pair_moves[3, h].wait_recv()
+        near_moves[1, h].wait_recv()
+        coded = mine(3, h) + from_pair[3, h].astype(f32) + from_near[1, h].astype(f32)
+        far_moves[h].wait_recv()
+        coded = coded + from_far[h].astype(f32)
+        here = pl.ds(h * (half // 2), half // 2)
+        new_first = beta_first * first_in[here] + (1.0 - beta_first) * coded
+        new_second = beta_second * second_in[here] + (1.0 - beta_second) * coded * coded
+        first_out[here] = new_first
+        second_out[here] = new_second
+        first_hat = new_first / (1.0 - beta_first**adam_steps)
+        second_hat = new_second / (1.0 - beta_second**adam_steps)
+        ratio = first_hat / (jnp.sqrt(second_hat) + adam_eps)
+        rows = []
+        for a in range(2):
+            if a:
+                mixed = ratio[:, :key_width] - ratio[:, key_width:]
+            else:
+                mixed = ratio[:, :key_width] + ratio[:, key_width:]
+            turned = jnp.zeros_like(mixed)
+            for _ in range(3):
+                high = mixed.astype(bf16)
+                mixed = mixed - high.astype(f32)
+                turned = turned + jnp.dot(high, had[...], preferred_element_type=f32)
+            rows.append(
+                (turned * (1.0 / norm_root) * sign_row[a]).reshape(
+                    half // (2 * PAIR_GAP), 1, PAIR_GAP, key_width
+                )
+            )
+        update = jnp.concatenate(rows, axis=1).reshape(master_half, key_width)
+        there = pl.ds(h * master_half, master_half)
+        old = master_in[there]
+        new_master = old - learn_rate * (update + weight_decay * old)
+        master_out[there] = new_master
+        sec_out[rep, there] = new_master.astype(bf16)
+        src = spread_block(rep, h)
+        for k in (2, 1):
+            spread_moves[k, h] = go(
+                remote(src, src, ss.at[k - 1, h], sr.at[k - 1, h], rep_peer[k])
+            )
+
+    def spread_on(h):
+        spread_moves[2, h].wait_recv()
+        src = spread_block(flip(rep, 2), h)
+        spread_moves[3, h] = go(remote(src, src, ss.at[2, h], sr.at[2, h], rep_peer[1]))
+
+    to_pair(0, 7)
+    local_grads()
+    arrived(4)
+    weight(4, 2)
+    keep(0, 6)
+    use_grads(1)
+    to_neighbour(0, 0)
+    to_pair(1, 3)
+    to_neighbour(0, 1)
+    use_grads(4)
+    keep(1, 2)
+    to_neighbour(1, 0)
+    to_pair(2, 5)
+    to_neighbour(1, 1)
+    keep(2, 4)
+    use_keys(4, True)
+    arrived(2)
+    use_keys(2)
+    to_distant(0)
+    to_pair(3, 1)
+    weight(4, 1)
+    use_keys(1)
+    to_distant(1)
+    weight(1, 2)
+    use_grads(6)
+    use_keys(6)
+    weight(6, 1)
+    fetch(0)
+    keep(3, 0)
+    use_keys(0)
+    for copy in state:
+        copy.wait()
+    finalize(0)
+    finalize(1)
+    use_grads(5)
+    use_keys(5)
     use_grads(3)
     use_keys(3)
-    put(total.at[1], make_term(7))
-    use_keys(0)
-    pairs[2].wait_recv()
-    near[0].wait_recv()
-    put(
-        to_far,
-        plus(halves(total.at[0]), plus(halves(from_pair.at[2]), halves(from_near.at[0]))),
-    )
-    far = go(remote(to_far, from_far, zs.at[2], zr.at[2], node_peer[4]))
-    pairs[3].wait_recv()
-    near[1].wait_recv()
-    put(
-        total.at[1],
-        plus(halves(total.at[1]), plus(halves(from_pair.at[3]), halves(from_near.at[1]))),
-    )
-    use_grads(5)
-    use_keys(5)
-
-    for copy in state:
-        copy.wait()
-    far.wait_recv()
-    coded = total[1] + from_far[...].astype(f32)
-    new_first = beta_first * first_in[...] + (1.0 - beta_first) * coded
-    new_second = beta_second * second_in[...] + (1.0 - beta_second) * coded * coded
-    first_out[...] = new_first
-    second_out[...] = new_second
-    first_hat = new_first / (1.0 - beta_first**adam_steps)
-    second_hat = new_second / (1.0 - beta_second**adam_steps)
-    ratio = first_hat / (jnp.sqrt(second_hat) + adam_eps)
-    norm_root = math.sqrt(2 * key_width)
-    rows = []
-    for a in range(2):
-        if a:
-            mixed = ratio[:, :key_width] - ratio[:, key_width:]
-        else:
-            mixed = ratio[:, :key_width] + ratio[:, key_width:]
-        turned = jnp.zeros_like(mixed)
-        for _ in range(3):
-            high = mixed.astype(bf16)
-            mixed = mixed - high.astype(f32)
-            turned = turned + jnp.dot(high, had[...], preferred_element_type=f32)
-        rows.append(
-            (turned * (1.0 / norm_root) * sign_row[a]).reshape(
-                half // PAIR_GAP, 1, PAIR_GAP, key_width
-            )
-        )
-    update = jnp.concatenate(rows, axis=1).reshape(columns, key_width)
-    new_master = master_in[...] - learn_rate * (update + weight_decay * master_in[...])
-    master_out[...] = new_master
-    sec_out[rep] = new_master.astype(bf16)
-    mine = sec_out.at[rep]
-    spread_moves = {
-        k: go(remote(mine, mine, ss.at[k - 1], sr.at[k - 1], rep_peer[k])) for k in (2, 1)
-    }
-
+    spread_on(0)
     use_grads(7)
     use_keys(7)
     for i, k in enumerate((3, 1)):
@@ -618,6 +678,9 @@
         acc[pl.ds(pl.multiple_of(away * tok_rows, tok_rows), tok_rows)] + part_in[0].astype(f32)
     ).astype(bf16)
     cross_move = go(remote(cross, cross_in, ks.at[1], kr.at[1], rep_peer[2]))
+    spread_on(1)
+    pass_on(0)
+    extra_grads(0)
 
     def overlap(node):
         def add(k, running):
@@ -645,17 +708,15 @@
 
     lax.fori_loop(0, pieces, finish, 0)
 
-    spread_moves[2].wait_recv()
-    across = sec_out.at[flip(rep, 2)]
-    spread_moves[3] = go(remote(across, across, ss.at[2], sr.at[2], rep_peer[1]))
     cross_move.wait_recv()
     keys_out[...] = (
         acc[pl.ds(pl.multiple_of(rep * tok_rows, tok_rows), tok_rows)]
         + part_in[1].astype(f32)
         + cross_in[...].astype(f32)
     ).astype(keys_out.dtype)
-    spread_moves[1].wait_recv()
-    spread_moves[3].wait_recv()
+    for k in (1, 3):
+        for h in range(2):
+            spread_moves[k, h].wait_recv()
     for copy in sent:
         copy.wait_send()
 
@@ -686,6 +747,7 @@
     columns = master.shape[0]
     pieces = model_width // columns
     block = first.shape
+    part = (block[0] // 2, block[1])
     group_tokens = reps * tok_rows
     vmem = pltpu.VMEM
     far = functools.partial(pltpu.with_memory_space_constraint, memory_space=pltpu.HBM)
@@ -710,13 +772,13 @@
             vmem(sec.shape, bf16),
             vmem((group_tokens, 2 * key_width), bf16),
             vmem((key_width, key_width), bf16),
-            vmem((4,) + block, bf16),
-            vmem((2,) + block, f32),
-            vmem((4,) + block, bf16),
-            vmem((2,) + block, bf16),
-            vmem((2,) + block, bf16),
-            vmem(block, bf16),
-            vmem(block, bf16),
+            vmem((4, 2) + part, bf16),
+            vmem((4,) + block, f32),
+            vmem((4, 2) + part, bf16),
+            vmem((2, 2) + part, bf16),
+            vmem((2, 2) + part, bf16),
+            vmem((2,) + part, bf16),
+            vmem((2,) + part, bf16),
             vmem((nodes, reps, tok_rows, columns), bf16),
             vmem((pieces, tok_rows, columns), bf16),
             vmem((group_tokens, key_width), f32),
@@ -728,16 +790,18 @@
             vmem(master.shape, f32),
             vmem(block, f32),
             vmem(block, f32),
+            vmem((2, 4, columns, key_width), bf16),
         ]
         + [dma((pieces,)), dma((5,))]
         + [dma((3,))] * 2
         + [dma((3, nodes))] * 2
         + [dma((nodes - 1,))] * 2
-        + [dma((4,))] * 2
-        + [dma((3,))] * 2
+        + [dma((4, 2))] * 2
+        + [dma((3, 2))] * 2
         + [dma((3, nodes))] * 2
         + [dma((2,))] * 2
-        + [dma((3,))] * 2,
+        + [dma((3, 2))] * 2
+        + [dma((2, 4))] * 2,
         compiler_params=pltpu.CompilerParams(
             collective_id=2, has_side_effects=True, vmem_limit_bytes=56 << 20
         ),

time: 68.4 us -> 64.2 us (0.939)
  Pallas kernels: 67.6 us -> 63.2 us
    pallas_call x1, Pallas kernels: 65.1 us -> 60.6 us  [fused(): pl.pallas_call(functools.partial(fused_kernel, nodes, reps, scale), out_s...]
where the time goes in v2:
time: 64.2 us; the launch traced here: 63.8 us
  Pallas kernels  63.2 us (98%)
    pallas_call x1, Pallas kernels, fused(): pl.pallas_call(functools.partial(fused_kernel, nodes, reps, scale), out_s...  60.6 us
    pallas_call x1, Pallas kernels, fused(): pl.pallas_call(store_kernel, out_shape=(like(cot.shape, bf16), like(token...  2.55 us

profile of v2, /device:TPU:0, one launch (start us, length us, event | category | flops | bytes accessed | tf_op | source)
XLA Modules:
  0.0 63.8 jit_solution(2932438418294095384)
XLA Ops:
  0.6 60.6 %shard_map.127 = (bf16[128,512]{1,0:T(8,128)(2,1)S(1)}, bf16[32,128,256]{2,1,0:T(8,128)(2,1)S(1)}, f32[256,512]{1,0:T(8,128)S(1)}, f32[128,1024]{1,0:T(8,128)S(1...) custom-call(bf16[128,8192]{1,0:T(8,128)(2,1)} %tok.1, f32[32,1,256]{2,1,0:T(1,128)} %bitcast.2, ...), custom_call_target="tpu_custom_call" | custom-call | tf_op jit(solution)/shard_map/pallas_call | solution.py:754
  61.3 2.5 %shard_map.128 = (bf16[128,512]{1,0:T(8,128)(2,1)}, bf16[128,8192]{1,0:T(8,128)(2,1)}, f32[256,512]{1,0:T(8,128)}, f32[128,1024]{1,0:T(8,128)}, f32[128,1024]{1,0:T(8,128)}, /*index=5*/bf16[1024,512]{1,0:T(8,128)(2,1)}) custom-call(bf16[128,512]{1,0:T(8,128)(2,1)S(1)} %get-tuple-element.12.keys, bf16[32,128,256]{2,1,0:T(8,128)(2,1)S(1)} %get-tuple-element.13.grad, ...), custom_call_target="tpu_custom_call" | custom-call | tf_op jit(solution)/shard_map/pallas_call | solution.py:814

commit v3 on v2

--- a/solution.py
+++ b/solution.py
@@ -329,11 +329,11 @@
 
 def fused_kernel(
     nodes, reps, scale,
-    tok, gain, cot, sec, master, first, second, signs,
+    tok, gain_hbm, cot, sec, master, first, second, signs_hbm,
     keys_out, grad_out, master_out, first_out, second_out, sec_out,
     x_in, hid, hid_in, cot_in, sec_in, sec_own, rot, had, term, total, from_pair,
-    to_near, from_near, to_far, from_far, grad, grad_in, acc, inv,
-    part, part_in, cross, cross_in, master_in, first_in, second_in, ext,
+    to_chain, from_chain, grad, grad_in, acc, inv,
+    part, part_in, cross, cross_in, master_in, first_in, second_in, ext, gain, signs,
     xl, ll, cs, cr, hs, hr, ws, wr, ps, pr, zs, zr, gs, gr, ks, kr, ss, sr, es, er,
 ):
     f32, bf16 = jnp.float32, jnp.bfloat16
@@ -345,7 +345,25 @@
     half = columns // 2
     rep_kinds = (2, 3, 1)
     rep_peer = {k: {"rep": flip(rep, k)} for k in rep_kinds}
-    node_peer = {k: {"node": flip(me, k)} for k in (1, 2, 4)}
+    level, side = split(me)
+    upper, odd = split(level)
+    inner = upper + odd - 2 * upper * odd
+    beside = {"node": flip(me, 1)}
+    next_to = {"node": flip(me, 2)}
+    middle = {"node": 2 * (nodes // 2 - 1 - level) + side}
+
+    def inside(body):
+        pl.when(inner == 1)(body)
+
+    def at_end(body):
+        pl.when(inner == 0)(body)
+
+    last = nodes // 2 - 1
+    source = [level + 1 - 2 * odd, 2 - upper, last - last * upper]
+    target = [last - last * upper, 2 + upper - 2 * odd, 1 + odd, level]
+
+    def node_at(z, other):
+        return 2 * z + (1 - side if other else side)
 
     loads = [
         pltpu.make_async_copy(tok.at[:, pl.ds(columns * i, columns)], x_in.at[i], xl.at[i])
@@ -358,42 +376,58 @@
         pltpu.make_async_copy(first, first_in, ll.at[3]),
         pltpu.make_async_copy(second, second_in, ll.at[4]),
     ]
-    for copy in loads + [own_cot, own_sec] + state:
+    small = [
+        pltpu.make_async_copy(gain_hbm, gain, ll.at[5]),
+        pltpu.make_async_copy(signs_hbm, signs, ll.at[6]),
+    ]
+    for copy in [own_cot] + loads + small + [own_sec] + state:
         copy.start()
-    greet([rep_peer[k] for k in rep_kinds] + [node_peer[k] for k in (1, 2, 4)])
+    barrier = pltpu.get_barrier_semaphore()
+    common = [rep_peer[k] for k in rep_kinds] + [beside, next_to]
+    for peer in common:
+        pl.semaphore_signal(barrier, inc=1, device_id=peer, device_id_type=MESH)
+
+    @inside
+    def _():
+        pl.semaphore_signal(barrier, inc=1, device_id=middle, device_id_type=MESH)
+
+    pl.semaphore_wait(barrier, len(common) + inner)
 
     sent = []
-
-    def go(copy):
+    sent_inside = []
+    sent_at_end = []
+
+    def go(copy, where=sent):
         copy.start()
-        sent.append(copy)
+        where.append(copy)
         return copy
 
     quarter = sec.at[pl.ds(pl.multiple_of(rep * columns, columns), columns)]
-    slots = {}
-
-    def weight(source, via):
-        slot = len(slots)
-        src = sec_in.at[flip(me, source)] if source else quarter
-        copy = remote(src, sec_in.at[flip(me, source)], ws.at[slot], wr.at[slot], node_peer[via])
-        slots[source ^ via] = go(copy)
-
-    held = set()
-
-    def arrived(bits):
-        if bits not in held:
-            held.add(bits)
-            slots[bits].wait_recv()
-
-    weight(0, 4)
-    weight(0, 1)
-    weight(0, 2)
+    counter = []
+
+    def weight(z, other, peer, slot, where=sent):
+        node = me if z is None else node_at(z, other)
+        src = quarter if z is None else sec_in.at[node]
+        index = len(counter)
+        counter.append(index)
+        copy = remote(src, sec_in.at[node], ws.at[index], wr.at[slot], peer)
+        where.append(copy)
+        return copy
+
+    def arrived(slot):
+        block = sec_in.at[me]
+        remote(block, block, ws.at[0], wr.at[slot], beside).wait_recv()
+
+    weight(None, 0, next_to, (0, 0)).start()
+    weight(None, 0, beside, (0, 3)).start()
+    inside(weight(None, 0, middle, (0, 1), sent_inside).start)
+
     cot_moves = {
         2: go(remote(cot, cot_in.at[rep], cs.at[0], cr.at[0], rep_peer[2])),
         1: go(remote(cot, cot_in.at[rep], cs.at[1], cr.at[1], rep_peer[1])),
     }
 
-    for copy in loads:
+    for copy in loads + small:
         copy.wait()
 
     def squares(i, running):
@@ -407,11 +441,9 @@
     mean = jnp.sum(squared, axis=-1, keepdims=True) * (1.0 / (pieces * columns))
     inv[...] = jnp.broadcast_to(lax.rsqrt(mean + norm_eps), inv.shape)
 
-    order = [7, 6, 3, 2, 5, 4, 1, 0]
-    place = {bits: i for i, bits in enumerate(order)}
+    order = [node_at(z, other) for z in target for other in (1, 0)]
     hid_moves = []
-    for i, bits in enumerate(order):
-        node = flip(me, bits)
+    for i, node in enumerate(order):
         moves = []
         for k in rep_kinds + (0,):
             owner = flip(rep, k)
@@ -454,10 +486,10 @@
             jnp.dot(flipped, had[...], preferred_element_type=f32) * scale
         ).astype(bf16)
 
-    def make_term(bits):
-        for copy in hid_moves[place[bits]]:
+    def make_term(i):
+        for copy in hid_moves[i]:
             copy.wait_recv()
-        chunk = hid_in[flip(me, bits)].reshape(group_tokens, columns)
+        chunk = hid_in[order[i]].reshape(group_tokens, columns)
         product = lax.dot_general(
             chunk, rot[...], (((0,), (0,)), ((), ())), preferred_element_type=f32
         ).reshape(columns // (2 * PAIR_GAP), 2, PAIR_GAP, 2 * key_width)
@@ -471,7 +503,7 @@
             value = value + other.astype(f32)
         dst[...] = value.astype(dst.dtype)
 
-    grad_moves = {}
+    grad_moves = []
 
     def local_grads():
         own_sec.wait()
@@ -480,18 +512,15 @@
             grad_in[me * reps + k] = lax.dot_general(
                 cot_in[rep], block, (((1,), (1,)), ((), ())), preferred_element_type=f32
             ).astype(bf16)
-        grad_moves[0] = []
-
-    def use_grads(bits):
-        arrived(bits)
-        node = flip(me, bits)
+
+    def use_grads(node):
         rows = lax.dot_general(
             cot_in[...].reshape(group_tokens, key_width), sec_in[node], (((1,), (1,)), ((), ())),
             preferred_element_type=f32,
         )
         grad[node] = rows.astype(bf16).reshape(reps, tok_rows, columns)
         slot = len(grad_moves)
-        grad_moves[bits] = [
+        moves = [
             go(
                 remote(
                     grad.at[node, flip(rep, k)], grad_in.at[node * reps + rep],
@@ -500,11 +529,14 @@
             )
             for k in rep_kinds
         ]
+        grad_moves.append((node, moves))
         grad_in[node * reps + rep] = grad[node, rep]
 
-    def use_keys(bits, start=False):
-        node = flip(me, bits)
-        block = sec_in[node] if bits else sec_own[pl.ds(pl.multiple_of(rep * columns, columns), columns)]
+    def use_keys(node, start=False):
+        if node is me:
+            block = sec_own[pl.ds(pl.multiple_of(rep * columns, columns), columns)]
+        else:
+            block = sec_in[node]
         product = jnp.dot(
             hid_in[node].reshape(group_tokens, columns), block, preferred_element_type=f32
         )
@@ -513,23 +545,21 @@
         else:
             acc[...] += product
 
-    near_nodes = (2,)
-    extra = {}
+    extra_nodes = [node_at(level, 1), node_at(source[0], 0)]
+    extra = [[], []]
 
     def fetch(e):
         other = sec.at[pl.ds(pl.multiple_of(flip(rep, 2) * columns, columns), columns)]
-        bits = near_nodes[e]
-        extra[e] = [go(remote(other, ext.at[e, 2], es.at[e, 2], er.at[e, 2], node_peer[bits]))]
+        peer = next_to if e else beside
+        extra[e].append(go(remote(other, ext.at[e, 2], es.at[e, 2], er.at[e, 2], peer)))
 
     def pass_on(e):
-        node = flip(me, near_nodes[e])
-        arrived(near_nodes[e])
         extra[e][0].wait_recv()
-        for k, src in ((1, sec_in.at[node]), (3, ext.at[e, 2])):
+        for k, src in ((1, sec_in.at[extra_nodes[e]]), (3, ext.at[e, 2])):
             extra[e].append(go(remote(src, ext.at[e, k], es.at[e, k], er.at[e, k], rep_peer[1])))
 
     def extra_grads(e):
-        node = flip(me, near_nodes[e])
+        node = extra_nodes[e]
         for copy in extra[e][1:]:
             copy.wait_recv()
         for k in range(4):
@@ -537,41 +567,50 @@
             grad_in[node * reps + flip(rep, k)] = lax.dot_general(
                 cot_in[rep], block, (((1,), (1,)), ((), ())), preferred_element_type=f32
             ).astype(bf16)
-        grad_moves[near_nodes[e]] = []
-
-    pair_moves, near_moves, far_moves = {}, {}, {}
-
-    def to_pair(i, bits):
-        upper, lower = make_term(bits)
-        rows = upper.shape[0] // 2
+
+    pair_moves = {}
+
+    def to_pair(i):
+        upper_half, lower_half = make_term(2 * i)
+        rows = upper_half.shape[0] // 2
         for h in range(2):
-            term[i, h, :, :key_width] = upper[h * rows : (h + 1) * rows].astype(bf16)
-            term[i, h, :, key_width:] = lower[h * rows : (h + 1) * rows].astype(bf16)
+            term[i, h, :, :key_width] = upper_half[h * rows : (h + 1) * rows].astype(bf16)
+            term[i, h, :, key_width:] = lower_half[h * rows : (h + 1) * rows].astype(bf16)
             pair_moves[i, h] = go(
-                remote(term.at[i, h], from_pair.at[i, h], ps.at[i, h], pr.at[i, h], node_peer[1])
+                remote(term.at[i, h], from_pair.at[i, h], ps.at[i, h], pr.at[i, h], beside)
             )
 
-    def keep(i, bits):
-        upper, lower = make_term(bits)
-        total[i, :, :key_width] = upper
-        total[i, :, key_width:] = lower
+    def keep(i):
+        upper_half, lower_half = make_term(2 * i + 1)
+        total[i, :, :key_width] = upper_half
+        total[i, :, key_width:] = lower_half
 
     def mine(i, h):
         rows = total.shape[1] // 2
         return total[i, h * rows : (h + 1) * rows]
 
-    def to_neighbour(i, h):
-        pair_moves[i, h].wait_recv()
-        add_up(to_near.at[i, h], mine(i, h), from_pair[i, h])
-        near_moves[i, h] = go(
-            remote(to_near.at[i, h], from_near.at[i, h], zs.at[i, h], zr.at[i, h], node_peer[2])
+    def chained(index, h):
+        dst = from_chain.at[index, h]
+        remote(dst, dst, zs.at[0, h], zr.at[index, h], next_to).wait_recv()
+        return from_chain[index, h]
+
+    def pass_sum(i, h, within):
+        other = middle if within else next_to
+        peer, index = [(other, within), (next_to, 2 + within), (other, 3 + within)][i]
+        copy = remote(
+            to_chain.at[i, h], from_chain.at[index, h], zs.at[i, h], zr.at[index, h], peer
         )
-
-    def to_distant(h):
-        pair_moves[2, h].wait_recv()
-        near_moves[0, h].wait_recv()
-        add_up(to_far.at[h], mine(2, h), from_pair[2, h], from_near[0, h])
-        far_moves[h] = go(remote(to_far.at[h], from_far.at[h], zs.at[2, h], zr.at[2, h], node_peer[4]))
+        (sent_inside if within else sent_at_end).append(copy)
+
+        def body():
+            pair_moves[i, h].wait_recv()
+            parts = [mine(i, h), from_pair[i, h]]
+            if within:
+                parts.append(chained(i, h))
+            add_up(to_chain.at[i, h], *parts)
+            copy.start()
+
+        (inside if within else at_end)(body)
 
     spread_moves = {}
     norm_root = math.sqrt(2 * key_width)
@@ -582,10 +621,16 @@
 
     def finalize(h):
         pair_moves[3, h].wait_recv()
-        near_moves[1, h].wait_recv()
-        coded = mine(3, h) + from_pair[3, h].astype(f32) + from_near[1, h].astype(f32)
-        far_moves[h].wait_recv()
-        coded = coded + from_far[h].astype(f32)
+        rows = total.shape[1] // 2
+        total[3, h * rows : (h + 1) * rows] = (
+            mine(3, h) + from_pair[3, h].astype(f32) + chained(3, h).astype(f32)
+        )
+
+        @inside
+        def _():
+            total[3, h * rows : (h + 1) * rows] += chained(4, h).astype(f32)
+
+        coded = mine(3, h)
         here = pl.ds(h * (half // 2), half // 2)
         new_first = beta_first * first_in[here] + (1.0 - beta_first) * coded
         new_second = beta_second * second_in[here] + (1.0 - beta_second) * coded * coded
@@ -627,47 +672,104 @@
         src = spread_block(flip(rep, 2), h)
         spread_moves[3, h] = go(remote(src, src, ss.at[2, h], sr.at[2, h], rep_peer[1]))
 
-    to_pair(0, 7)
+    to_pair(0)
     local_grads()
-    arrived(4)
-    weight(4, 2)
-    keep(0, 6)
-    use_grads(1)
-    to_neighbour(0, 0)
-    to_pair(1, 3)
-    to_neighbour(0, 1)
-    use_grads(4)
-    keep(1, 2)
-    to_neighbour(1, 0)
-    to_pair(2, 5)
-    to_neighbour(1, 1)
-    keep(2, 4)
-    use_keys(4, True)
-    arrived(2)
-    use_keys(2)
-    to_distant(0)
-    to_pair(3, 1)
-    weight(4, 1)
-    use_keys(1)
-    to_distant(1)
-    weight(1, 2)
-    use_grads(6)
-    use_keys(6)
-    weight(6, 1)
+    arrived((0, 0))
+
+    first_on = weight(source[0], 0, middle, (0, 2), sent_inside)
+    second_on = weight(source[1], 0, next_to, (0, 1), sent_inside)
+
+    @inside
+    def _():
+        first_on.start()
+        arrived((0, 1))
+        second_on.start()
+
+    arrived((0, 3))
+    at_end(weight(level, 1, next_to, (1, 0), sent_at_end).start)
+
+    keep(0)
+    pass_sum(0, 0, 0)
+    to_pair(1)
+    pass_sum(0, 1, 0)
+
+    onwards = [
+        weight(source[2], 0, next_to, (0, 2), sent_inside),
+        weight(level, 1, next_to, (1, 0), sent_inside),
+        weight(level, 1, middle, (1, 1), sent_inside),
+    ]
+
+    @inside
+    def _():
+        arrived((0, 2))
+        for copy in onwards:
+            copy.start()
+
+    keep(1)
+    pass_sum(0, 0, 1)
+    pass_sum(1, 0, 0)
+
+    @at_end
+    def _():
+        arrived((0, 1))
+
+    use_grads(node_at(source[1], 0))
+    to_pair(2)
+    pass_sum(0, 1, 1)
+    pass_sum(1, 1, 0)
+    keep(2)
+    use_keys(node_at(source[0], 0), True)
+    use_keys(node_at(source[1], 0))
+    pass_sum(1, 0, 1)
+    pass_sum(2, 0, 0)
+    to_pair(3)
+    pass_sum(1, 1, 1)
+    pass_sum(2, 1, 0)
+
+    sideways = weight(source[2], 0, beside, (1, 2), sent_at_end)
+
+    @at_end
+    def _():
+        arrived((0, 2))
+        sideways.start()
+
     fetch(0)
-    keep(3, 0)
-    use_keys(0)
+    use_grads(node_at(source[2], 0))
+    pass_sum(2, 0, 1)
+    arrived((1, 0))
+    use_grads(node_at(source[0], 1))
+    pass_sum(2, 1, 1)
+
+    third_on = weight(source[0], 1, middle, (1, 2), sent_inside)
+    fourth_on = weight(source[1], 1, next_to, (1, 1), sent_inside)
+
+    @inside
+    def _():
+        third_on.start()
+        arrived((1, 1))
+        fourth_on.start()
+
+    fetch(1)
+    keep(3)
+    use_keys(node_at(source[2], 0))
+    use_keys(node_at(level, 1))
+    use_keys(me)
+    use_keys(node_at(source[0], 1))
     for copy in state:
         copy.wait()
     finalize(0)
     finalize(1)
-    use_grads(5)
-    use_keys(5)
-    use_grads(3)
-    use_keys(3)
+
+    @at_end
+    def _():
+        arrived((1, 1))
+
+    use_grads(node_at(source[1], 1))
+    use_keys(node_at(source[1], 1))
     spread_on(0)
-    use_grads(7)
-    use_keys(7)
+    arrived((1, 2))
+    use_grads(node_at(source[2], 1))
+    use_keys(node_at(source[2], 1))
     for i, k in enumerate((3, 1)):
         owner = flip(rep, k)
         part[i] = acc[pl.ds(pl.multiple_of(owner * tok_rows, tok_rows), tok_rows)].astype(bf16)
@@ -679,8 +781,10 @@
     ).astype(bf16)
     cross_move = go(remote(cross, cross_in, ks.at[1], kr.at[1], rep_peer[2]))
     spread_on(1)
-    pass_on(0)
-    extra_grads(0)
+    for e in range(2):
+        pass_on(e)
+    for e in range(2):
+        extra_grads(e)
 
     def overlap(node):
         def add(k, running):
@@ -693,10 +797,10 @@
         return add
 
     running = jnp.zeros((tok_rows, 128), f32)
-    for bits, moves in grad_moves.items():
+    for node, moves in [(node, []) for node in [me] + extra_nodes] + grad_moves:
         for copy in moves:
             copy.wait_recv()
-        running = lax.fori_loop(0, reps, overlap(flip(me, bits)), running)
+        running = lax.fori_loop(0, reps, overlap(node), running)
     against = jnp.sum(running, axis=-1, keepdims=True) * (1.0 / (pieces * columns))
     one = inv[:, :1]
     factor = jnp.broadcast_to(one * one * one * against, (tok_rows, columns))
@@ -708,6 +812,10 @@
 
     lax.fori_loop(0, pieces, finish, 0)
 
+    late = [cross_move] + [spread_moves[3, h] for h in range(2)]
+    for copy in sent:
+        if not any(copy is other for other in late):
+            copy.wait_send()
     cross_move.wait_recv()
     keys_out[...] = (
         acc[pl.ds(pl.multiple_of(rep * tok_rows, tok_rows), tok_rows)]
@@ -717,8 +825,18 @@
     for k in (1, 3):
         for h in range(2):
             spread_moves[k, h].wait_recv()
-    for copy in sent:
+    for copy in late:
         copy.wait_send()
+
+    @inside
+    def _():
+        for copy in sent_inside:
+            copy.wait_send()
+
+    @at_end
+    def _():
+        for copy in sent_at_end:
+            copy.wait_send()
 
 
 def store_kernel(keys, grad, master, first, second, sec, *refs):
@@ -761,7 +879,7 @@
             vmem(block, f32),
             vmem((reps,) + master.shape, bf16),
         ),
-        in_specs=[HBM, VMEM, HBM, HBM, HBM, HBM, HBM, VMEM],
+        in_specs=[HBM] * 8,
         out_specs=(VMEM,) * 6,
         scratch_shapes=[
             vmem((pieces, tok_rows, columns), bf16),
@@ -775,10 +893,8 @@
             vmem((4, 2) + part, bf16),
             vmem((4,) + block, f32),
             vmem((4, 2) + part, bf16),
-            vmem((2, 2) + part, bf16),
-            vmem((2, 2) + part, bf16),
-            vmem((2,) + part, bf16),
-            vmem((2,) + part, bf16),
+            vmem((3, 2) + part, bf16),
+            vmem((5, 2) + part, bf16),
             vmem((nodes, reps, tok_rows, columns), bf16),
             vmem((pieces, tok_rows, columns), bf16),
             vmem((group_tokens, key_width), f32),
@@ -791,13 +907,15 @@
             vmem(block, f32),
             vmem(block, f32),
             vmem((2, 4, columns, key_width), bf16),
+            vmem((pieces, 1, columns), f32),
+            vmem((2 * key_width // 128, 128), jnp.int32),
         ]
-        + [dma((pieces,)), dma((5,))]
+        + [dma((pieces,)), dma((7,))]
         + [dma((3,))] * 2
         + [dma((3, nodes))] * 2
-        + [dma((nodes - 1,))] * 2
+        + [dma((12,)), dma((2, 4))]
         + [dma((4, 2))] * 2
-        + [dma((3, 2))] * 2
+        + [dma((3, 2)), dma((5, 2))]
         + [dma((3, nodes))] * 2
         + [dma((2,))] * 2
         + [dma((3, 2))] * 2
@@ -806,8 +924,8 @@
             collective_id=2, has_side_effects=True, vmem_limit_bytes=56 << 20
         ),
     )(
-        far(tokens), gain.reshape(pieces, 1, columns), far(cot), far(sec), far(master),
-        far(first), far(second), signs.reshape(-1, 128),
+        far(tokens), far(gain.reshape(pieces, 1, columns)), far(cot), far(sec), far(master),
+        far(first), far(second), far(signs.reshape(-1, 128)),
     )
     held = [pltpu.with_memory_space_constraint(value, pltpu.VMEM) for value in results]
     like = jax.ShapeDtypeStruct

time: 64.2 us -> 61.3 us (0.955)
  Pallas kernels: 63.2 us -> 60.5 us
    pallas_call x1, Pallas kernels: 60.6 us -> 57.9 us  [fused(): pl.pallas_call(functools.partial(fused_kernel, nodes, reps, scale), out_s...]
where the time goes in v3:
time: 61.3 us; the launch traced here: 61.1 us
  Pallas kernels  60.5 us (99%)
  between operations  0.64 us (1%)
    pallas_call x1, Pallas kernels, fused(): pl.pallas_call(functools.partial(fused_kernel, nodes, reps, scale), out_s...  57.9 us
    pallas_call x1, Pallas kernels, fused(): pl.pallas_call(store_kernel, out_shape=(like(cot.shape, bf16), like(token...  2.55 us

profile of v3, /device:TPU:0, one launch (start us, length us, event | category | flops | bytes accessed | tf_op | source)
XLA Modules:
  0.0 61.1 jit_solution(4968147034066312027)
XLA Ops:
  0.6 57.9 %shard_map.127 = (bf16[128,512]{1,0:T(8,128)(2,1)S(1)}, bf16[32,128,256]{2,1,0:T(8,128)(2,1)S(1)}, f32[256,512]{1,0:T(8,128)S(1)}, f32[128,1024]{1,0:T(8,128)S(1...) custom-call(bf16[128,8192]{1,0:T(8,128)(2,1)} %tok.1, f32[32,1,256]{2,1,0:T(1,128)} %bitcast.2, ...), custom_call_target="tpu_custom_call" | custom-call | tf_op jit(solution)/shard_map/pallas_call | solution.py:872
  58.6 2.5 %shard_map.128 = (bf16[128,512]{1,0:T(8,128)(2,1)}, bf16[128,8192]{1,0:T(8,128)(2,1)}, f32[256,512]{1,0:T(8,128)}, f32[128,1024]{1,0:T(8,128)}, f32[128,1024]{1,0:T(8,128)}, /*index=5*/bf16[1024,512]{1,0:T(8,128)(2,1)}) custom-call(bf16[128,512]{1,0:T(8,128)(2,1)S(1)} %get-tuple-element.12.keys, bf16[32,128,256]{2,1,0:T(8,128)(2,1)S(1)} %get-tuple-element.13.grad, ...), custom_call_target="tpu_custom_call" | custom-call | tf_op jit(solution)/shard_map/pallas_call | solution.py:932

commit v4 on v3

--- a/solution.py
+++ b/solution.py
@@ -330,10 +330,10 @@
 def fused_kernel(
     nodes, reps, scale,
     tok, gain_hbm, cot, sec, master, first, second, signs_hbm,
-    keys_out, grad_out, master_out, first_out, second_out, sec_out,
-    x_in, hid, hid_in, cot_in, sec_in, sec_own, rot, had, term, total, from_pair,
-    to_chain, from_chain, grad, grad_in, acc, inv,
-    part, part_in, cross, cross_in, master_in, first_in, second_in, ext, gain, signs,
+    keys_out, grad_in, master_out, first_out, second_out, sec_out, x_in, gain, inv, factor,
+    hid, hid_in, cot_in, sec_in, sec_own, rot, had, term, total, from_pair,
+    to_chain, from_chain, grad, acc,
+    part, part_in, cross, cross_in, master_in, first_in, second_in, ext, signs,
     xl, ll, cs, cr, hs, hr, ws, wr, ps, pr, zs, zr, gs, gr, ks, kr, ss, sr, es, er,
 ):
     f32, bf16 = jnp.float32, jnp.bfloat16
@@ -404,6 +404,16 @@
 
     quarter = sec.at[pl.ds(pl.multiple_of(rep * columns, columns), columns)]
     counter = []
+    extra = [[], []]
+
+    def fetch(e, h):
+        start = pl.multiple_of(flip(rep, 2) * columns + h * half, half)
+        peer = next_to if e else beside
+        dst = ext.at[e, 2, pl.ds(h * half, half)]
+        slot = 2 * h
+        extra[e].append(
+            go(remote(sec.at[pl.ds(start, half)], dst, es.at[e, slot], er.at[e, slot], peer))
+        )
 
     def weight(z, other, peer, slot, where=sent):
         node = me if z is None else node_at(z, other)
@@ -421,6 +431,8 @@
     weight(None, 0, next_to, (0, 0)).start()
     weight(None, 0, beside, (0, 3)).start()
     inside(weight(None, 0, middle, (0, 1), sent_inside).start)
+    for e in range(2):
+        fetch(e, 0)
 
     cot_moves = {
         2: go(remote(cot, cot_in.at[rep], cs.at[0], cr.at[0], rep_peer[2])),
@@ -546,21 +558,15 @@
             acc[...] += product
 
     extra_nodes = [node_at(level, 1), node_at(source[0], 0)]
-    extra = [[], []]
-
-    def fetch(e):
-        other = sec.at[pl.ds(pl.multiple_of(flip(rep, 2) * columns, columns), columns)]
-        peer = next_to if e else beside
-        extra[e].append(go(remote(other, ext.at[e, 2], es.at[e, 2], er.at[e, 2], peer)))
-
     def pass_on(e):
-        extra[e][0].wait_recv()
+        for copy in extra[e]:
+            copy.wait_recv()
         for k, src in ((1, sec_in.at[extra_nodes[e]]), (3, ext.at[e, 2])):
             extra[e].append(go(remote(src, ext.at[e, k], es.at[e, k], er.at[e, k], rep_peer[1])))
 
     def extra_grads(e):
         node = extra_nodes[e]
-        for copy in extra[e][1:]:
+        for copy in extra[e][2:]:
             copy.wait_recv()
         for k in range(4):
             block = ext[e, k] if k else sec_in[node]
@@ -722,19 +728,21 @@
     use_keys(node_at(source[1], 0))
     pass_sum(1, 0, 1)
     pass_sum(2, 0, 0)
+
+    @at_end
+    def _():
+        arrived((0, 2))
+
+    use_grads(node_at(source[2], 0))
     to_pair(3)
     pass_sum(1, 1, 1)
     pass_sum(2, 1, 0)
 
     sideways = weight(source[2], 0, beside, (1, 2), sent_at_end)
 
-    @at_end
-    def _():
-        arrived((0, 2))
-        sideways.start()
-
-    fetch(0)
-    use_grads(node_at(source[2], 0))
+    at_end(sideways.start)
+
+    fetch(0, 1)
     pass_sum(2, 0, 1)
     arrived((1, 0))
     use_grads(node_at(source[0], 1))
@@ -749,7 +757,7 @@
         arrived((1, 1))
         fourth_on.start()
 
-    fetch(1)
+    fetch(1, 1)
     keep(3)
     use_keys(node_at(source[2], 0))
     use_keys(node_at(level, 1))
@@ -760,16 +768,19 @@
     finalize(0)
     finalize(1)
 
+    sooner = node_at(inner * source[1] + (1 - inner) * source[2], 1)
+    later = node_at(inner * source[2] + (1 - inner) * source[1], 1)
+
     @at_end
     def _():
-        arrived((1, 1))
-
-    use_grads(node_at(source[1], 1))
-    use_keys(node_at(source[1], 1))
+        arrived((1, 2))
+
+    use_grads(sooner)
+    use_keys(sooner)
     spread_on(0)
-    arrived((1, 2))
-    use_grads(node_at(source[2], 1))
-    use_keys(node_at(source[2], 1))
+    arrived((1, 2 * inner + 1 - inner))
+    use_grads(later)
+    use_keys(later)
     for i, k in enumerate((3, 1)):
         owner = flip(rep, k)
         part[i] = acc[pl.ds(pl.multiple_of(owner * tok_rows, tok_rows), tok_rows)].astype(bf16)
@@ -803,14 +814,7 @@
         running = lax.fori_loop(0, reps, overlap(node), running)
     against = jnp.sum(running, axis=-1, keepdims=True) * (1.0 / (pieces * columns))
     one = inv[:, :1]
-    factor = jnp.broadcast_to(one * one * one * against, (tok_rows, columns))
-
-    def finish(i, carry):
-        scaled = grad_in[i].astype(f32) * gain[i]
-        grad_out[i] = (inv[...] * scaled - x_in[i].astype(f32) * factor).astype(bf16)
-        return carry
-
-    lax.fori_loop(0, pieces, finish, 0)
+    factor[...] = jnp.broadcast_to(one * one * one * against, factor.shape)
 
     late = [cross_move] + [spread_moves[3, h] for h in range(2)]
     for copy in sent:
@@ -839,20 +843,26 @@
             copy.wait_send()
 
 
-def store_kernel(keys, grad, master, first, second, sec, *refs):
-    keys_out, grad_out, master_out, first_out, second_out, sec_out, sems = refs
+def store_kernel(keys, grad, master, first, second, sec, x, gain, inv, factor, *refs):
+    keys_out, grad_out, master_out, first_out, second_out, sec_out, done, sems = refs
     pieces, _, columns = grad.shape
     rows = sec.shape[1]
-    moves = [
-        pltpu.make_async_copy(grad.at[i], grad_out.at[:, pl.ds(columns * i, columns)], sems.at[i])
-        for i in range(pieces)
-    ]
     pairs = [(keys, keys_out), (master, master_out), (first, first_out), (second, second_out)]
     pairs += [(sec.at[i], sec_out.at[pl.ds(rows * i, rows)]) for i in range(sec.shape[0])]
-    for i, (src, dst) in enumerate(pairs):
-        moves.append(pltpu.make_async_copy(src, dst, sems.at[pieces + i]))
+    moves = [
+        pltpu.make_async_copy(src, dst, sems.at[pieces + i]) for i, (src, dst) in enumerate(pairs)
+    ]
     for copy in moves:
         copy.start()
+    for i in range(pieces):
+        scaled = grad[i].astype(jnp.float32) * gain[i]
+        done[i] = (inv[...] * scaled - x[i].astype(jnp.float32) * factor[...]).astype(done.dtype)
+        moves.append(
+            pltpu.make_async_copy(
+                done.at[i], grad_out.at[:, pl.ds(columns * i, columns)], sems.at[i]
+            )
+        )
+        moves[-1].start()
     for copy in moves:
         copy.wait()
 
@@ -878,11 +888,14 @@
             vmem(block, f32),
             vmem(block, f32),
             vmem((reps,) + master.shape, bf16),
+            vmem((pieces, tok_rows, columns), bf16),
+            vmem((pieces, 1, columns), f32),
+            vmem((tok_rows, columns), f32),
+            vmem((tok_rows, columns), f32),
         ),
         in_specs=[HBM] * 8,
-        out_specs=(VMEM,) * 6,
+        out_specs=(VMEM,) * 10,
         scratch_shapes=[
-            vmem((pieces, tok_rows, columns), bf16),
             vmem((nodes, reps, tok_rows, columns), bf16),
             vmem((nodes, reps, tok_rows, columns), bf16),
             vmem((reps, tok_rows, key_width), bf16),
@@ -896,9 +909,7 @@
             vmem((3, 2) + part, bf16),
             vmem((5, 2) + part, bf16),
             vmem((nodes, reps, tok_rows, columns), bf16),
-            vmem((pieces, tok_rows, columns), bf16),
             vmem((group_tokens, key_width), f32),
-            vmem((tok_rows, columns), f32),
             vmem((2, tok_rows, key_width), bf16),
             vmem((2, tok_rows, key_width), bf16),
             vmem((tok_rows, key_width), bf16),
@@ -907,7 +918,6 @@
             vmem(block, f32),
             vmem(block, f32),
             vmem((2, 4, columns, key_width), bf16),
-            vmem((pieces, 1, columns), f32),
             vmem((2 * key_width // 128, 128), jnp.int32),
         ]
         + [dma((pieces,)), dma((7,))]
@@ -921,7 +931,7 @@
         + [dma((3, 2))] * 2
         + [dma((2, 4))] * 2,
         compiler_params=pltpu.CompilerParams(
-            collective_id=2, has_side_effects=True, vmem_limit_bytes=56 << 20
+            collective_id=2, has_side_effects=True, vmem_limit_bytes=48 << 20
         ),
     )(
         far(tokens), far(gain.reshape(pieces, 1, columns)), far(cot), far(sec), far(master),
@@ -939,10 +949,10 @@
             like(block, f32),
             like(sec.shape, bf16),
         ),
-        in_specs=[VMEM] * 6,
+        in_specs=[VMEM] * 10,
         out_specs=(ANY,) * 6,
-        scratch_shapes=[dma((pieces + 4 + reps,))],
-        compiler_params=pltpu.CompilerParams(vmem_limit_bytes=1 << 20),
+        scratch_shapes=[vmem((pieces, tok_rows, columns), bf16), dma((pieces + 4 + reps,))],
+        compiler_params=pltpu.CompilerParams(vmem_limit_bytes=6 << 20),
     )(*held)
 
 

time: 61.3 us -> 59.3 us (0.967)
  Pallas kernels: 60.5 us -> 58.5 us
    pallas_call x1, Pallas kernels: 57.9 us -> 55.9 us  [fused(): pl.pallas_call(functools.partial(fused_kernel, nodes, reps, scale), out_s...]
where the time goes in v4:
time: 59.3 us; the launch traced here: 59.1 us
  Pallas kernels  58.5 us (99%)
  between operations  0.64 us (1%)
    pallas_call x1, Pallas kernels, fused(): pl.pallas_call(functools.partial(fused_kernel, nodes, reps, scale), out_s...  55.9 us
    pallas_call x1, Pallas kernels, fused(): pl.pallas_call(store_kernel, out_shape=(like(cot.shape, bf16), like(token...  2.53 us

profile of v4, /device:TPU:0, one launch (start us, length us, event | category | flops | bytes accessed | tf_op | source)
XLA Modules:
  0.0 59.1 jit_solution(9026189920396116130)
XLA Ops:
  0.6 55.9 %shard_map.127 = (bf16[128,512]{1,0:T(8,128)(2,1)S(1)}, bf16[32,128,256]{2,1,0:T(8,128)(2,1)S(1)}, f32[256,512]{1,0:T(8,128)S(1)}, f32[128,1024]{1,0:T(8,128)S(1...) custom-call(bf16[128,8192]{1,0:T(8,128)(2,1)} %tok.1, ...), custom_call_target="tpu_custom_call" | custom-call | tf_op jit(solution)/shard_map/pallas_call | solution.py:882
  56.6 2.5 %shard_map.128 = (bf16[128,512]{1,0:T(8,128)(2,1)}, bf16[128,8192]{1,0:T(8,128)(2,1)}, f32[256,512]{1,0:T(8,128)}, f32[128,1024]{1,0:T(8,128)}, f32[128,1024]{1,0:T(8,128)}, /*index=5*/bf16[1024,512]{1,0:T(8,128)(2,1)}) custom-call(bf16[128,512]{1,0:T(8,128)(2,1)S(1)} %get-tuple-element.16.keys, bf16[32,128,256]{2,1,0:T(8,128)(2,1)S(1)} %get-tuple-element.17.grad, ...), custom_call_target="tpu_custom_call" | custom-call | tf_op jit(solution)/shard_map/pallas_call | solution.py:942

commit v5 on v4

--- a/solution.py
+++ b/solution.py
@@ -333,8 +333,8 @@
     keys_out, grad_in, master_out, first_out, second_out, sec_out, x_in, gain, inv, factor,
     hid, hid_in, cot_in, sec_in, sec_own, rot, had, term, total, from_pair,
     to_chain, from_chain, grad, acc,
-    part, part_in, cross, cross_in, master_in, first_in, second_in, ext, signs,
-    xl, ll, cs, cr, hs, hr, ws, wr, ps, pr, zs, zr, gs, gr, ks, kr, ss, sr, es, er,
+    part, part_in, cross, cross_in, master_in, first_in, second_in, ext, ext_half, signs,
+    xl, ll, cs, cr, hs, hr, ws, wr, ps, pr, zs, zr, gs, gr, ks, kr, ss, sr, es, er, fs, fr,
 ):
     f32, bf16 = jnp.float32, jnp.bfloat16
     rep = lax.axis_index("rep")
@@ -525,22 +525,21 @@
                 cot_in[rep], block, (((1,), (1,)), ((), ())), preferred_element_type=f32
             ).astype(bf16)
 
-    def use_grads(node):
+    def use_grads(node, cut=False):
         rows = lax.dot_general(
             cot_in[...].reshape(group_tokens, key_width), sec_in[node], (((1,), (1,)), ((), ())),
             preferred_element_type=f32,
         )
         grad[node] = rows.astype(bf16).reshape(reps, tok_rows, columns)
         slot = len(grad_moves)
-        moves = [
-            go(
-                remote(
-                    grad.at[node, flip(rep, k)], grad_in.at[node * reps + rep],
-                    gs.at[k - 1, slot], gr.at[k - 1, slot], rep_peer[k],
-                )
+        moves = []
+        for k in rep_kinds:
+            src, dst = grad.at[node, flip(rep, k)], grad_in.at[node * reps + rep]
+            if cut and k > 1:
+                src, dst = src.at[:, pl.ds(half, half)], dst.at[:, pl.ds(half, half)]
+            moves.append(
+                go(remote(src, dst, gs.at[k - 1, slot], gr.at[k - 1, slot], rep_peer[k]))
             )
-            for k in rep_kinds
-        ]
         grad_moves.append((node, moves))
         grad_in[node * reps + rep] = grad[node, rep]
 
@@ -559,7 +558,7 @@
 
     extra_nodes = [node_at(level, 1), node_at(source[0], 0)]
     def pass_on(e):
-        for copy in extra[e]:
+        for copy in extra[e][e:]:
             copy.wait_recv()
         for k, src in ((1, sec_in.at[extra_nodes[e]]), (3, ext.at[e, 2])):
             extra[e].append(go(remote(src, ext.at[e, k], es.at[e, k], er.at[e, k], rep_peer[1])))
@@ -572,6 +571,27 @@
             block = ext[e, k] if k else sec_in[node]
             grad_in[node * reps + flip(rep, k)] = lax.dot_general(
                 cot_in[rep], block, (((1,), (1,)), ((), ())), preferred_element_type=f32
+            ).astype(bf16)
+
+    half_moves = []
+
+    def fetch_half():
+        extra[1][0].wait_recv()
+        src = ext.at[1, 2, pl.ds(0, half)]
+        half_moves.append(go(remote(src, ext_half.at[0], fs.at[0], fr.at[0], beside)))
+
+    def pass_half():
+        half_moves[0].wait_recv()
+        half_moves.append(
+            go(remote(ext_half.at[0], ext_half.at[1], fs.at[1], fr.at[1], rep_peer[1]))
+        )
+
+    def half_grads():
+        node = node_at(source[0], 1)
+        half_moves[1].wait_recv()
+        for i, k in enumerate((2, 3)):
+            grad_in[node * reps + flip(rep, k), :, :half] = lax.dot_general(
+                cot_in[rep], ext_half[i], (((1,), (1,)), ((), ())), preferred_element_type=f32
             ).astype(bf16)
 
     pair_moves = {}
@@ -693,23 +713,28 @@
 
     arrived((0, 3))
     at_end(weight(level, 1, next_to, (1, 0), sent_at_end).start)
+    across_on = [
+        weight(level, 1, middle, (1, 1), sent_inside),
+        weight(level, 1, next_to, (1, 0), sent_inside),
+    ]
+
+    @inside
+    def _():
+        for copy in across_on:
+            copy.start()
+
 
     keep(0)
     pass_sum(0, 0, 0)
     to_pair(1)
     pass_sum(0, 1, 0)
 
-    onwards = [
-        weight(source[2], 0, next_to, (0, 2), sent_inside),
-        weight(level, 1, next_to, (1, 0), sent_inside),
-        weight(level, 1, middle, (1, 1), sent_inside),
-    ]
+    fifth_on = weight(source[2], 0, next_to, (0, 2), sent_inside)
 
     @inside
     def _():
         arrived((0, 2))
-        for copy in onwards:
-            copy.start()
+        fifth_on.start()
 
     keep(1)
     pass_sum(0, 0, 1)
@@ -728,24 +753,24 @@
     use_keys(node_at(source[1], 0))
     pass_sum(1, 0, 1)
     pass_sum(2, 0, 0)
+    arrived((1, 0))
+    use_grads(node_at(source[0], 1), True)
+    to_pair(3)
+    pass_sum(2, 0, 1)
+    pass_sum(1, 1, 1)
+    pass_sum(2, 1, 0)
+
+    sideways = weight(source[2], 0, beside, (1, 2), sent_at_end)
 
     @at_end
     def _():
         arrived((0, 2))
 
     use_grads(node_at(source[2], 0))
-    to_pair(3)
-    pass_sum(1, 1, 1)
-    pass_sum(2, 1, 0)
-
-    sideways = weight(source[2], 0, beside, (1, 2), sent_at_end)
-
     at_end(sideways.start)
 
     fetch(0, 1)
-    pass_sum(2, 0, 1)
-    arrived((1, 0))
-    use_grads(node_at(source[0], 1))
+    fetch_half()
     pass_sum(2, 1, 1)
 
     third_on = weight(source[0], 1, middle, (1, 2), sent_inside)
@@ -794,8 +819,10 @@
     spread_on(1)
     for e in range(2):
         pass_on(e)
+    pass_half()
     for e in range(2):
         extra_grads(e)
+    half_grads()
 
     def overlap(node):
         def add(k, running):
@@ -918,6 +945,7 @@
             vmem(block, f32),
             vmem(block, f32),
             vmem((2, 4, columns, key_width), bf16),
+            vmem((2, columns // 2, key_width), bf16),
             vmem((2 * key_width // 128, 128), jnp.int32),
         ]
         + [dma((pieces,)), dma((7,))]
@@ -929,7 +957,8 @@
         + [dma((3, nodes))] * 2
         + [dma((2,))] * 2
         + [dma((3, 2))] * 2
-        + [dma((2, 4))] * 2,
+        + [dma((2, 4))] * 2
+        + [dma((2,))] * 2,
         compiler_params=pltpu.CompilerParams(
             collective_id=2, has_side_effects=True, vmem_limit_bytes=48 << 20
         ),

time: 59.3 us -> 58.3 us (0.983)
  Pallas kernels: 58.5 us -> 57.5 us
    pallas_call x1, Pallas kernels: 55.9 us -> 55 us  [fused(): pl.pallas_call(functools.partial(fused_kernel, nodes, reps, scale), out_s...]
where the time goes in v5:
time: 58.3 us; the launch traced here: 58.2 us
  Pallas kernels  57.5 us (99%)
  between operations  0.64 us (1%)
    pallas_call x1, Pallas kernels, fused(): pl.pallas_call(functools.partial(fused_kernel, nodes, reps, scale), out_s...  55 us
    pallas_call x1, Pallas kernels, fused(): pl.pallas_call(store_kernel, out_shape=(like(cot.shape, bf16), like(token...  2.53 us

profile of v5, /device:TPU:0, one launch (start us, length us, event | category | flops | bytes accessed | tf_op | source)
XLA Modules:
  0.0 58.2 jit_solution(4093216846919551688)
XLA Ops:
  0.6 55.0 %shard_map.127 = (bf16[128,512]{1,0:T(8,128)(2,1)S(1)}, bf16[32,128,256]{2,1,0:T(8,128)(2,1)S(1)}, f32[256,512]{1,0:T(8,128)S(1)}, f32[128,1024]{1,0:T(8,128)S(1...) custom-call(bf16[128,8192]{1,0:T(8,128)(2,1)} %tok.1, ...), custom_call_target="tpu_custom_call" | custom-call | tf_op jit(solution)/shard_map/pallas_call | solution.py:909
  55.6 2.5 %shard_map.128 = (bf16[128,512]{1,0:T(8,128)(2,1)}, bf16[128,8192]{1,0:T(8,128)(2,1)}, f32[256,512]{1,0:T(8,128)}, f32[128,1024]{1,0:T(8,128)}, f32[128,1024]{1,0:T(8,128)}, /*index=5*/bf16[1024,512]{1,0:T(8,128)(2,1)}) custom-call(bf16[128,512]{1,0:T(8,128)(2,1)S(1)} %get-tuple-element.16.keys, bf16[32,128,256]{2,1,0:T(8,128)(2,1)S(1)} %get-tuple-element.17.grad, ...), custom_call_target="tpu_custom_call" | custom-call | tf_op jit(solution)/shard_map/pallas_call | solution.py:971

commit v6 on v5

--- a/solution.py
+++ b/solution.py
@@ -810,6 +810,24 @@
         owner = flip(rep, k)
         part[i] = acc[pl.ds(pl.multiple_of(owner * tok_rows, tok_rows), tok_rows)].astype(bf16)
     part_move = go(remote(part, part_in, ks.at[0], kr.at[0], rep_peer[1]))
+    def overlap(node):
+        def add(k, running):
+            index = node * reps + k
+            value = grad_in[index].astype(f32) * gain[index] * x_in[index].astype(f32)
+            for lane in range(0, columns, 128):
+                running = running + value[:, lane : lane + 128]
+            return running
+
+        return add
+
+    def collect(running, node, moves):
+        for copy in moves:
+            copy.wait_recv()
+        return lax.fori_loop(0, reps, overlap(node), running)
+
+    running = jnp.zeros((tok_rows, 128), f32)
+    for entry in [(me, []), grad_moves[0], grad_moves[2]]:
+        running = collect(running, *entry)
     part_move.wait_recv()
     away = flip(rep, 2)
     cross[...] = (
@@ -824,21 +842,8 @@
         extra_grads(e)
     half_grads()
 
-    def overlap(node):
-        def add(k, running):
-            index = node * reps + k
-            value = grad_in[index].astype(f32) * gain[index] * x_in[index].astype(f32)
-            for lane in range(0, columns, 128):
-                running = running + value[:, lane : lane + 128]
-            return running
-
-        return add
-
-    running = jnp.zeros((tok_rows, 128), f32)
-    for node, moves in [(node, []) for node in [me] + extra_nodes] + grad_moves:
-        for copy in moves:
-            copy.wait_recv()
-        running = lax.fori_loop(0, reps, overlap(node), running)
+    for entry in [(node, []) for node in extra_nodes] + grad_moves[1:2] + grad_moves[3:]:
+        running = collect(running, *entry)
     against = jnp.sum(running, axis=-1, keepdims=True) * (1.0 / (pieces * columns))
     one = inv[:, :1]
     factor[...] = jnp.broadcast_to(one * one * one * against, factor.shape)

time: 58.3 us -> 58.3 us (level)
  no operation moved by 1% of the time
where the time goes in v6:
time: 58.3 us; the launch traced here: 58.2 us
  Pallas kernels  57.5 us (99%)
  between operations  0.64 us (1%)
    pallas_call x1, Pallas kernels, fused(): pl.pallas_call(functools.partial(fused_kernel, nodes, reps, scale), out_s...  55 us
    pallas_call x1, Pallas kernels, fused(): pl.pallas_call(store_kernel, out_shape=(like(cot.shape, bf16), like(token...  2.53 us

profile of v6, /device:TPU:0, one launch (start us, length us, event | category | flops | bytes accessed | tf_op | source)
XLA Modules:
  0.0 58.2 jit_solution(11461210836272269555)
XLA Ops:
  0.6 55.0 %shard_map.127 = (bf16[128,512]{1,0:T(8,128)(2,1)S(1)}, bf16[32,128,256]{2,1,0:T(8,128)(2,1)S(1)}, f32[256,512]{1,0:T(8,128)S(1)}, f32[128,1024]{1,0:T(8,128)S(1...) custom-call(bf16[128,8192]{1,0:T(8,128)(2,1)} %tok.1, ...), custom_call_target="tpu_custom_call" | custom-call | tf_op jit(solution)/shard_map/pallas_call | solution.py:914
  55.6 2.5 %shard_map.128 = (bf16[128,512]{1,0:T(8,128)(2,1)}, bf16[128,8192]{1,0:T(8,128)(2,1)}, f32[256,512]{1,0:T(8,128)}, f32[128,1024]{1,0:T(8,128)}, f32[128,1024]{1,0:T(8,128)}, /*index=5*/bf16[1024,512]{1,0:T(8,128)(2,1)}) custom-call(bf16[128,512]{1,0:T(8,128)(2,1)S(1)} %get-tuple-element.16.keys, bf16[32,128,256]{2,1,0:T(8,128)(2,1)S(1)} %get-tuple-element.17.grad, ...), custom_call_target="tpu_custom_call" | custom-call | tf_op jit(solution)/shard_map/pallas_call | solution.py:976
